TPU v7x, 128 devices: a whole 4x4x4 slice. The times are simulated.
128 devices in a mesh: lat: 8 (over x, core), lon: 16 (over y, z).
Axes of the slice: x: 4, y: 4, z: 4, core: 2. Of those that a mesh axis runs over, the one named last changes fastest.
Arguments:
- nodes: bfloat16 [8, 16, 384, 512], P('lat', 'lon'), may hold values from -6 to 6
- edges: bfloat16 [8, 16, 3072, 512], P('lat', 'lon'), may hold values from -6 to 6
- senders: int32 [8, 16, 3072], P('lat', 'lon'), may hold values from 0 to 607, as said below
- receivers: int32 [8, 16, 3072], P('lat', 'lon'), may hold values from 0 to 383
- edge_count: int32 [8, 16], P('lat', 'lon'), may hold values from 1536 to 3072, as said below
- halo_send: int32 [8, 16, 4, 24], P('lat', 'lon'), may hold values from 0 to 383
- long_need: int32 [8, 16, 128, 1], P('lat', 'lon'), may hold values from 0 to 1
- node_cot: bfloat16 [8, 16, 384, 512], P('lat', 'lon'), may hold values from -6 to 6
- edge_cot: bfloat16 [8, 16, 3072, 512], P('lat', 'lon'), may hold values from -6 to 6
- e_w1: bfloat16 [1536, 512], replicated, may hold values from -0.15625 to 0.15625
- e_b1: float32 [512], replicated, may hold values from -3 to 3
- e_w2: bfloat16 [512, 512], replicated, may hold values from -0.25 to 0.25
- e_gain: float32 [512], replicated, may hold values from 0.25 to 1.75
- n_w1: bfloat16 [1024, 512], replicated, may hold values from -0.1875 to 0.1875
- n_b1: float32 [512], replicated, may hold values from -3 to 3
- n_w2: bfloat16 [512, 512], replicated, may hold values from -0.25 to 0.25
- n_gain: float32 [512], replicated, may hold values from 0.25 to 1.75
Outputs:
- new_nodes: bfloat16 [8, 16, 384, 512], P('lat', 'lon')
- new_edges: bfloat16 [8, 16, 3072, 512], P('lat', 'lon')
- node_grad: float32 [8, 16, 384, 512], P('lat', 'lon')
- edge_grad: float32 [8, 16, 3072, 512], P('lat', 'lon')
- e_w1_grad: float32 [1536, 512], P(('lat', 'lon'))
- e_b1_grad: float32 [512], P(('lat', 'lon'))
- e_w2_grad: float32 [512, 512], P(('lat', 'lon'))
- e_gain_grad: float32 [512], P(('lat', 'lon'))
- n_w1_grad: float32 [1024, 512], P(('lat', 'lon'))
- n_b1_grad: float32 [512], P(('lat', 'lon'))
- n_w2_grad: float32 [512, 512], P(('lat', 'lon'))
- n_gain_grad: float32 [512], P(('lat', 'lon'))
Inputs may be any that keep to these rules, and one draw needn't show every extreme that they name: `senders`: entries below 384 are a region's own nodes, the next 96 the four neighbour blocks, the rest the coarse rows; the third block is never named in the first band and the fourth never in the last. The first three edge slots of region r name the coarse rows of regions r + 1, r - 1 and r + 64 in flat order, counted round. `edge_count`: some region has all 3072 slots live. `long_need`: A region's coarse nodes are its first 2 rows.
All inputs are finite; a program needn't handle non-finite values.
Results may differ from a plain program's by a relative error of at most 0.009.
Values may be sent and summed in bfloat16 or wider, within the bound.
No kernel may reach another device: no remote copies, remote signals or barrier semaphores. Data moves between devices by JAX's collectives and lax.ppermute only.
A program may use at most 192 MiB of HBM per device.

v0:
```python
import functools

import jax
import jax.numpy as jnp
from jax import lax
from jax.experimental import pallas as pl
from jax.experimental.pallas import tpu as pltpu
from jax.sharding import Mesh
from jax.sharding import PartitionSpec as P

COARSE = 2
LON = ("lon_0", "lon_1")
LAT = ("lat_0", "lat_1")
LAT_LON = ("lat_0", "lat_1", "lon_0", "lon_1")
EPS = 1e-05
BF = jnp.bfloat16
F32 = jnp.float32

NODES = 384
HALO = 24
WIDE = 512
EDGES = 3072
FAR = 128
BLOCK = 768
STEPS = EDGES // BLOCK
SENDERS = 640
ONES_ROW = 608
TABLE = SENDERS + NODES
FIRST = WIDE + SENDERS
GROUPS = 32
GROUP_ROWS = 128


def mm(a, b):
    return lax.dot_general(a, b, (((1,), (0,)), ((), ())), preferred_element_type=F32)


def mm_t(a, b):
    return lax.dot_general(a, b, (((1,), (1,)), ((), ())), preferred_element_type=F32)


def t_mm(a, b):
    return lax.dot_general(a, b, (((0,), (0,)), ((), ())), preferred_element_type=F32)


def row_mean(v):
    return jnp.sum(v, axis=1, keepdims=True) * (1.0 / WIDE)


def first_act(z):
    sig = 0.5 + 0.5 * jnp.tanh(0.5 * z)
    act = z * sig
    return act, sig + act * (1.0 - sig)


def normalise(z):
    centred = z - row_mean(z)
    rstd = lax.rsqrt(row_mean(centred * centred) + EPS)
    return centred * rstd, rstd


def norm_back(g, normed, rstd, gain):
    s = g * gain
    return rstd * (s - row_mean(s) - normed * row_mean(s * normed))


def lane_ids(row):
    return jnp.transpose(jnp.broadcast_to(row, (128, BLOCK)))


def hot_lanes(ids, first, chunks):
    lane = lax.broadcasted_iota(jnp.int32, (BLOCK, 128), 1).astype(F32)
    return [
        jnp.where(ids == lane + float(first + 128 * j), 1.0, 0.0).astype(BF) for j in range(chunks)
    ]


def spread_kernel(nodes_ref, coarse_ref):
    coarse_ref[...] = jnp.broadcast_to(nodes_ref[0:COARSE][None], (FAR, COARSE, WIDE))


def spread(nodes):
    return pl.pallas_call(
        spread_kernel,
        name="spread_coarse",
        grid=(1,),
        in_specs=[pl.BlockSpec((16, WIDE), lambda i: (0, 0))],
        out_specs=pl.BlockSpec((FAR, COARSE, WIDE), lambda i: (0, 0, 0)),
        out_shape=jax.ShapeDtypeStruct((FAR, COARSE, WIDE), BF),
    )(nodes)


def border_kernel(nodes_ref, rows_ref, *sent_refs):
    at = lax.broadcasted_iota(jnp.int32, (NODES, HALO), 0)
    for k, sent_ref in enumerate(sent_refs):
        hot = jnp.where(at == rows_ref[k : k + 1], 1.0, 0.0).astype(BF)
        sent_ref[...] = t_mm(hot, nodes_ref[...]).astype(BF)


def borders(nodes, rows_out):
    return pl.pallas_call(
        border_kernel,
        name="border_rows",
        out_shape=[jax.ShapeDtypeStruct((HALO, WIDE), BF)] * 4,
        cost_estimate=pl.CostEstimate(
            flops=8 << 30, transcendentals=0, bytes_accessed=8 << 20
        ),
    )(nodes, rows_out)


def whole(*shape):
    return pl.BlockSpec(shape, lambda i: (0,) * len(shape), pipeline_mode=pl.Buffered(1))


def by_block(shape, pick):
    return pl.BlockSpec(shape, lambda i: (pick(i),) + (0,) * (len(shape) - 1))


def params():
    return pltpu.CompilerParams(
        dimension_semantics=("arbitrary",), vmem_limit_bytes=60 * 1024 * 1024
    )


def layer_kernel(
    place_ref,
    snd_ref,
    rcv_ref,
    need_ref,
    edges_ref,
    ecot_ref,
    nodes_ref,
    from_east_ref,
    from_west_ref,
    from_north_ref,
    from_south_ref,
    far_ref,
    ncot_ref,
    ew1_ref,
    ew2_ref,
    nw1_ref,
    nw2_ref,
    eb1_ref,
    eg_ref,
    nb1_ref,
    ng_ref,
    new_nodes_ref,
    new_edges_ref,
    gz_ref,
    gagg_ref,
    node_ref,
    east_ref,
    west_ref,
    north_ref,
    south_ref,
    keep_ref,
    send_ref,
    table_s,
    right_s,
    left_s,
    act_s,
    dact_s,
    normed_s,
    rstd_s,
    agg_s,
    gnode_s,
    dw1_s,
    dw2_s,
    gain_s,
    nvec_s,
    packed_s,
    sems,
):
    step = pl.program_id(0)
    count = place_ref[0]
    egain = eg_ref[...].reshape(1, WIDE)

    def out_copies(g):
        copies = []
        for other, ref in ((0, keep_ref), (1, send_ref)):
            group = (g >> 2) * 8 + (place_ref[1] ^ other) * 4 + (g & 3)
            copies.append(
                pltpu.make_async_copy(packed_s.at[group], ref.at[g], sems.at[2 * g + other])
            )
        return copies

    @pl.when(step == 0)
    def _():
        table_s[0:NODES] = nodes_ref[...]
        borders = (from_east_ref, from_west_ref, from_north_ref, from_south_ref)
        table_s[NODES : NODES + 96] = jnp.concatenate(
            [ref[...].astype(F32) for ref in borders], axis=0
        ).astype(BF)
        need = need_ref[...].astype(F32)
        pick = jnp.transpose(jnp.broadcast_to(need, (128, 128)))[:, 0:1]
        low, high = far_ref[:, 0].astype(F32), far_ref[:, 1].astype(F32)
        table_s[480:608] = jnp.where(pick == 0.0, low, high).astype(BF)
        table_s[608:SENDERS] = jnp.zeros((32, WIDE), BF)
        right_s[0:WIDE] = ew1_ref[0:WIDE]
        right_s[WIDE:FIRST] = mm(table_s[...], ew1_ref[WIDE : 2 * WIDE]).astype(BF)
        right_s[FIRST:] = mm(nodes_ref[...], ew1_ref[2 * WIDE :]).astype(BF)
        agg_s[...] = jnp.zeros_like(agg_s)
        dw1_s[...] = jnp.zeros_like(dw1_s)
        dw2_s[...] = jnp.zeros_like(dw2_s)
        gain_s[...] = jnp.zeros_like(gain_s)

    @pl.when(step < STEPS)
    def _():
        at = pl.multiple_of(step * BLOCK, BLOCK)
        here = pl.ds(at, BLOCK)
        slot = lax.broadcasted_iota(jnp.int32, (1, BLOCK), 1) + at
        snd = snd_ref[0].astype(F32)
        rcv = jnp.where(slot < count, rcv_ref[0].astype(F32), -1.0)
        edges = edges_ref[...]
        left_s[here, 0:WIDE] = edges
        hots = hot_lanes(lane_ids(snd), 0, SENDERS // 128)
        lane = lax.broadcasted_iota(jnp.int32, (BLOCK, 128), 1)
        hots[4] = jnp.where(lane == ONES_ROW - 512, 1.0, hots[4].astype(F32)).astype(BF)
        hots += hot_lanes(lane_ids(rcv), 0, NODES // 128)
        for k, hot in enumerate(hots):
            left_s[here, WIDE + 128 * k : WIDE + 128 * (k + 1)] = hot
        z1 = mm(left_s[here], right_s[...]) + eb1_ref[...].reshape(1, WIDE)
        act, dact = first_act(z1)
        act = act.astype(BF)
        act_s[here] = act
        dact_s[here] = dact.astype(BF)
        normed, rstd = normalise(mm(act, ew2_ref[...]))
        normed_s[here] = normed.astype(BF)
        rstd_s[here] = jnp.broadcast_to(rstd, (BLOCK, 128))
        live = (lax.broadcasted_iota(jnp.int32, (BLOCK, 1), 0) + at < count).astype(F32)
        fresh = (edges.astype(F32) + (live * normed) * egain).astype(BF)
        new_edges_ref[...] = fresh
        agg_s[...] += t_mm(left_s[here, FIRST:], fresh)

    @pl.when(step == STEPS - 1)
    def _():
        nodes = nodes_ref[...]
        ngain = ng_ref[...].reshape(1, WIDE)
        agg = agg_s[...].astype(BF)
        z1 = mm(nodes, nw1_ref[0:WIDE]) + mm(agg, nw1_ref[WIDE:]) + nb1_ref[...].reshape(1, WIDE)
        act, dact = first_act(z1)
        act = act.astype(BF)
        normed, rstd = normalise(mm(act, nw2_ref[...]))
        new_nodes_ref[...] = (nodes.astype(F32) + normed * ngain).astype(BF)
        cot = ncot_ref[...].astype(F32)
        gz2 = norm_back(cot, normed, rstd, ngain).astype(BF)
        nvec_s[1:2] = jnp.sum(cot * normed, axis=0, keepdims=True)
        gz1 = (mm_t(gz2, nw2_ref[...]) * dact).astype(BF)
        nvec_s[0:1] = jnp.sum(gz1.astype(F32), axis=0, keepdims=True)
        packed_s[0:16, 0:32] = t_mm(nodes, gz1).astype(BF).reshape(16, 32, WIDE)
        packed_s[16:32, 0:32] = t_mm(agg, gz1).astype(BF).reshape(16, 32, WIDE)
        packed_s[:, 32:48] = t_mm(act, gz2).astype(BF).reshape(GROUPS, 16, WIDE)
        gnode_s[...] = cot + mm_t(gz1, nw1_ref[0:WIDE])
        gagg_ref[...] = mm_t(gz1, nw1_ref[WIDE:]).astype(BF)

    @pl.when(step >= STEPS)
    def _():
        at = pl.multiple_of((step - STEPS) * BLOCK, BLOCK)
        here = pl.ds(at, BLOCK)
        live = (lax.broadcasted_iota(jnp.int32, (BLOCK, 1), 0) + at < count).astype(F32)
        g = live * ecot_ref[...].astype(F32) + mm(left_s[here, FIRST:], gagg_ref[...])
        normed = normed_s[here].astype(F32)
        gain_s[...] += jnp.sum((g * normed).reshape(BLOCK // 8, 8, WIDE), axis=0)
        gz2 = norm_back(g, normed, rstd_s[here][:, 0:1], egain).astype(BF)
        dw2_s[...] += t_mm(act_s[here], gz2)
        gz1 = (mm_t(gz2, ew2_ref[...]) * dact_s[here].astype(F32)).astype(BF)
        gz_ref[...] = gz1
        dw1_s[...] += t_mm(left_s[here], gz1)

    @pl.when(step == 2 * STEPS - 1)
    def _():
        packed_s[:, 96:112] = dw2_s[...].astype(BF).reshape(GROUPS, 16, WIDE)
        sent, got = dw1_s[WIDE:FIRST].astype(BF), dw1_s[FIRST:].astype(BF)
        first = jnp.concatenate(
            [
                dw1_s[0:WIDE].astype(BF),
                t_mm(table_s[...], sent).astype(BF),
                t_mm(nodes_ref[...], got).astype(BF),
            ],
            axis=0,
        )
        packed_s[:, 48:96] = first.reshape(GROUPS, 48, WIDE)
        back = mm_t(sent, ew1_ref[WIDE : 2 * WIDE])
        vectors = (
            dw1_s[WIDE + ONES_ROW : WIDE + ONES_ROW + 1],
            jnp.sum(gain_s[...], axis=0, keepdims=True),
            nvec_s[0:1],
            nvec_s[1:2],
        )
        half = WIDE // 2
        paired = [
            jnp.concatenate([vectors[k][:, side], vectors[k + 1][:, side]], axis=1)
            for side in (slice(0, half), slice(half, WIDE))
            for k in (0, 2)
        ]
        extra = jnp.concatenate([back[480:608]] + paired + [jnp.zeros((124, WIDE), F32)], axis=0)
        out = lax.broadcasted_iota(jnp.int32, (GROUPS * 16, 256), 0)
        src = lax.broadcasted_iota(jnp.int32, (GROUPS * 16, 256), 1)
        need = jnp.concatenate([need_ref[...], jnp.zeros((1, 128), jnp.int32)], axis=1)
        slot = out & 15
        low = (slot < 4) & (src == (out >> 4) * 4 + slot) & (need == 0)
        high = (slot >= 4) & (slot < 8) & (src == (out >> 4) * 4 + slot - 4) & (need == 1)
        small = (slot >= 8) & (slot < 10) & (src == 120 + slot + (out >> 8) * 2)
        move = jnp.where(low | high | small, 1.0, 0.0).astype(BF)
        packed_s[:, 112:128] = mm(move, extra.astype(BF)).astype(BF).reshape(GROUPS, 16, WIDE)
        out = lax.broadcasted_iota(jnp.int32, (128, 128), 0)
        src = lax.broadcasted_iota(jnp.int32, (128, 128), 1)
        z, slot = out >> 5, out & 31
        want = jnp.where(slot < 8, 8 * z + slot, 24 + 4 * z + slot)
        want = jnp.where(slot >= 12, 36 + 12 * z + slot, want)
        want = jnp.where(slot >= 24, 72 + 4 * z + slot, want)
        want = jnp.where(slot >= 28, 112 + z + 4 * (slot - 28), want)
        want = jnp.where(slot >= 30, 90 + slot, want)
        order = jnp.where(src == want, 1.0, 0.0).astype(BF)
        for g in range(16):
            for group in ((g >> 2) * 8 + (g & 3), (g >> 2) * 8 + 4 + (g & 3)):
                packed_s[group] = mm(order, packed_s[group]).astype(BF)
            for copy in out_copies(g):
                copy.start()
        node_ref[...] = gnode_s[...] + back[0:NODES] + mm_t(got, ew1_ref[2 * WIDE :])
        for k, ref in enumerate((east_ref, west_ref, north_ref, south_ref)):
            ref[...] = back[NODES + HALO * k : NODES + HALO * (k + 1)].astype(BF)
        for g in range(16):
            for copy in out_copies(g):
                copy.wait()


def layer(place, snd, rcv, need, edges, ecot, nodes, borders, far, ncot, ew1, ew2, nw1, nw2, eb1, eg, nb1, ng):
    first = lambda i: jnp.minimum(i, STEPS - 1)
    later = lambda i: jnp.maximum(i - STEPS, 0)
    sds = jax.ShapeDtypeStruct
    return pl.pallas_call(
        layer_kernel,
        name="mesh_layer",
        grid=(2 * STEPS,),
        in_specs=[
            pl.BlockSpec(memory_space=pltpu.SMEM),
            by_block((1, 1, BLOCK), first),
            by_block((1, 1, BLOCK), first),
            whole(1, FAR),
            by_block((BLOCK, WIDE), first),
            by_block((BLOCK, WIDE), later),
            whole(NODES, WIDE),
            whole(HALO, WIDE),
            whole(HALO, WIDE),
            whole(HALO, WIDE),
            whole(HALO, WIDE),
            whole(FAR, COARSE, WIDE),
            whole(NODES, WIDE),
            whole(3 * WIDE, WIDE),
            whole(WIDE, WIDE),
            whole(2 * WIDE, WIDE),
            whole(WIDE, WIDE),
            whole(WIDE),
            whole(WIDE),
            whole(WIDE),
            whole(WIDE),
        ],
        out_specs=[
            whole(NODES, WIDE),
            by_block((BLOCK, WIDE), first),
            by_block((BLOCK, WIDE), later),
            whole(NODES, WIDE),
            whole(NODES, WIDE),
        ]
        + [whole(HALO, WIDE)] * 4
        + [pl.BlockSpec(memory_space=pl.ANY)] * 2,
        out_shape=[
            sds((NODES, WIDE), BF),
            sds((EDGES, WIDE), BF),
            sds((EDGES, WIDE), BF),
            sds((NODES, WIDE), BF),
            sds((NODES, WIDE), F32),
        ]
        + [sds((HALO, WIDE), BF)] * 4
        + [sds((16, GROUP_ROWS, WIDE), BF)] * 2,
        scratch_shapes=[
            pltpu.VMEM((SENDERS, WIDE), BF),
            pltpu.VMEM((WIDE + TABLE, WIDE), BF),
            pltpu.VMEM((EDGES, WIDE + TABLE), BF),
            pltpu.VMEM((EDGES, WIDE), BF),
            pltpu.VMEM((EDGES, WIDE), BF),
            pltpu.VMEM((EDGES, WIDE), BF),
            pltpu.VMEM((EDGES, 128), F32),
            pltpu.VMEM((NODES, WIDE), F32),
            pltpu.VMEM((NODES, WIDE), F32),
            pltpu.VMEM((WIDE + TABLE, WIDE), F32),
            pltpu.VMEM((WIDE, WIDE), F32),
            pltpu.VMEM((8, WIDE), F32),
            pltpu.VMEM((8, WIDE), F32),
            pltpu.VMEM((GROUPS, GROUP_ROWS, WIDE), BF),
            pltpu.SemaphoreType.DMA((32,)),
        ],
        compiler_params=params(),
        cost_estimate=pl.CostEstimate(
            flops=18 << 30, transcendentals=4 << 20, bytes_accessed=30 << 20
        ),
    )(place, snd, rcv, need, edges, ecot, nodes, *borders, far, ncot, ew1, ew2, nw1, nw2, eb1, eg, nb1, ng)


def edge_grad_kernel(count_ref, rcv_ref, ecot_ref, gz_ref, gagg_ref, ew1_ref, out_ref):
    at = pl.program_id(0) * BLOCK
    back = jnp.concatenate(hot_lanes(lane_ids(rcv_ref[0].astype(F32)), 0, NODES // 128), axis=1)
    live = (lax.broadcasted_iota(jnp.int32, (BLOCK, 1), 0) + at < count_ref[0]).astype(F32)
    taken = live * mm(back, gagg_ref[...])
    out_ref[...] = ecot_ref[...].astype(F32) + taken + mm_t(gz_ref[...], ew1_ref[...])


def edge_grads(place, rcv, ecot, gz, gagg, ew1):
    same = lambda i: i
    return pl.pallas_call(
        edge_grad_kernel,
        name="edge_grads",
        grid=(STEPS,),
        in_specs=[
            pl.BlockSpec(memory_space=pltpu.SMEM),
            by_block((1, 1, BLOCK), same),
            by_block((BLOCK, WIDE), same),
            by_block((BLOCK, WIDE), same),
            whole(NODES, WIDE),
            whole(WIDE, WIDE),
        ],
        out_specs=by_block((BLOCK, WIDE), same),
        out_shape=jax.ShapeDtypeStruct((EDGES, WIDE), F32),
        compiler_params=params(),
        cost_estimate=pl.CostEstimate(
            flops=2 * EDGES * WIDE * (WIDE + NODES), transcendentals=0, bytes_accessed=13 << 20
        ),
    )(place, rcv, ecot, gz, gagg, ew1)


def finish_kernel(lane_ref, total_ref, node_ref, out_ref, *grads):
    total = total_ref[...]
    ew1, eb1, ew2, eg, nw1, nb1, nw2, ng = grads
    nw1[...] = total[0:8]
    nw2[...] = total[8:12]
    ew1[...] = total[12:24]
    ew2[...] = total[24:28]
    out_ref[...] = node_ref[...]
    out_ref[0:COARSE] += total[28:30]
    half = WIDE // 2
    lines = [total[30:31, :half], total[30:31, half:], total[31:32, :half], total[31:32, half:]]
    lines = jnp.concatenate(lines + [jnp.zeros((4, half), F32)], axis=0)
    lines = pltpu.roll(lines, (half - lane_ref[0]) & (half - 1), 1)
    for k, ref in enumerate((eb1, eg, nb1, ng)):
        ref[...] = lines[k, 0:4]


def finish(lane, total, node_grad):
    sds = jax.ShapeDtypeStruct
    rows = [(12, WIDE), (4,), (4, WIDE), (4,), (8, WIDE), (4,), (4, WIDE), (4,)]
    first = pl.BlockSpec((8, WIDE), lambda i: (0, 0))
    return pl.pallas_call(
        finish_kernel,
        name="finish_grads",
        grid=(1,),
        in_specs=[
            pl.BlockSpec(memory_space=pltpu.SMEM),
            whole(GROUP_ROWS // 4, WIDE),
            first,
        ],
        out_specs=[first] + [pl.BlockSpec(r, lambda i, n=len(r): (0,) * n) for r in rows],
        out_shape=[sds((NODES, WIDE), F32)] + [sds(r, F32) for r in rows],
        input_output_aliases={2: 0},
        compiler_params=params(),
    )(lane, total, node_grad)


def ring(block, axis, distance):
    n = lax.axis_size(axis)
    return lax.ppermute(block, axis, [(i, (i + distance) % n) for i in range(n)])


def passed_along(value, axis, steps):
    count = lax.axis_size(axis)
    leading, last = (max(0, -steps), min(count, count - steps))
    return lax.ppermute(value, axis, [(source, source + steps) for source in range(leading, last)])


def shards(
    nodes,
    edges,
    senders,
    receivers,
    edge_count,
    halo_send,
    long_need,
    node_cot,
    edge_cot,
    e_w1,
    e_b1,
    e_w2,
    e_gain,
    n_w1,
    n_b1,
    n_w2,
    n_gain,
):
    nodes_l, edges_l, ecot = nodes[0, 0], edges[0, 0], edge_cot[0, 0]
    rows_out = halo_send[0, 0]
    snd = senders.reshape(STEPS, 1, BLOCK)
    rcv = receivers.reshape(STEPS, 1, BLOCK)
    far = lax.all_to_all(spread(nodes_l), LAT_LON, split_axis=0, concat_axis=0, tiled=True)
    sent = borders(nodes_l, rows_out)
    halo = [
        ring(sent[0], LON, 1),
        ring(sent[1], LON, -1),
        passed_along(sent[2], LAT, 1),
        passed_along(sent[3], LAT, -1),
    ]
    place = jnp.stack([edge_count[0, 0], lax.axis_index("lat_1").astype(jnp.int32)])
    new_nodes, new_edges, gz, gagg, node_part, *rest = layer(
        place,
        snd,
        rcv,
        long_need.reshape(1, FAR),
        edges_l,
        ecot,
        nodes_l,
        halo,
        far,
        node_cot[0, 0],
        e_w1,
        e_w2,
        n_w1,
        n_w2,
        e_b1,
        e_gain,
        n_b1,
        n_gain,
    )
    halo_grad, (keep, send) = rest[:4], rest[4:]
    pair = lax.ppermute(send, "lat_1", [(0, 1), (1, 0)])
    both = (keep.astype(F32) + pair.astype(F32)).astype(BF).reshape(64, GROUP_ROWS // 4, WIDE)
    both, halo_grad, gz = lax.optimization_barrier((both, halo_grad, gz))
    parts = lax.all_to_all(
        both, ("lat_0", "lon_0", "lon_1"), split_axis=0, concat_axis=0, tiled=True
    )
    edge_grad = edge_grads(place, rcv, ecot, gz, gagg, e_w1)
    returned = [
        ring(halo_grad[0], LON, -1),
        ring(halo_grad[1], LON, 1),
        passed_along(halo_grad[2], LAT, -1),
        passed_along(halo_grad[3], LAT, 1),
    ]
    border = (rows_out.reshape(1, 4 * HALO) == lax.broadcasted_iota(jnp.int32, (NODES, 4 * HALO), 0)).astype(BF)
    node_grad = node_part + jnp.dot(border, jnp.concatenate(returned, axis=0), preferred_element_type=F32)
    parts, edge_grad, node_grad = lax.optimization_barrier((parts, edge_grad, node_grad))
    lane = ((lax.axis_index(LAT_LON) & 63) * 4).astype(jnp.int32).reshape(1)
    node_grad, *sums = finish(lane, jnp.sum(parts.astype(F32), axis=0), node_grad)
    return (
        new_nodes[None, None],
        new_edges[None, None],
        node_grad[None, None],
        edge_grad[None, None],
        *sums,
    )


def solution(mesh):
    finer = Mesh(mesh.devices.reshape(4, 2, 4, 4), ("lat_0", "lat_1", "lon_0", "lon_1"))
    placed = (
        P(LAT, LON, None, None),
        P(LAT, LON, None, None),
        P(LAT, LON, None),
        P(LAT, LON, None),
        P(LAT, LON),
        P(LAT, LON, None, None),
        P(LAT, LON, None, None),
        P(LAT, LON, None, None),
        P(LAT, LON, None, None),
        P(),
        P(),
        P(),
        P(),
        P(),
        P(),
        P(),
        P(),
    )
    return jax.shard_map(
        shards,
        mesh=finer,
        in_specs=placed,
        out_specs=(
            P(LAT, LON, None, None),
            P(LAT, LON, None, None),
            P(LAT, LON, None, None),
            P(LAT, LON, None, None),
            P(LAT_LON, None),
            P(LAT_LON),
            P(LAT_LON, None),
            P(LAT_LON),
            P(LAT_LON, None),
            P(LAT_LON),
            P(LAT_LON, None),
            P(LAT_LON),
        ),
        check_vma=False,
    )
```

profile of v0, /device:TPU:0, one launch (start us, length us, event | category | flops | bytes accessed | tf_op | source)
XLA Modules:
  0.0 115.9 jit_solution(10806513204448013557)
XLA Ops:
  0.6 1.5 %spread_coarse.1 = bf16[128,2,512]{2,1,0:T(2,128)(2,1)} custom-call(bf16[384,512]{1,0:T(8,128)(2,1)} %bitcast.21), custom_call_target="tpu_custom_call" | custom-call | tf_op jit(solution)/shard_map/spread_coarse/pallas_call | solution.py:83
  2.1 11.1 %all-to-all-start = ((bf16[128,2,512]{2,1,0:T(2,128)(2,1)}), bf16[128,2,512]{2,1,0:T(2,128)(2,1)S(1)}, u32[]{:S(2)}, u32[]{:S(2)}) async-start(bf16[128,2,512]{2,1,0:T(2,128)(2,1)} %spread_coarse.1), calls=%async_computation | async-start | bytes 524288 | tf_op jit(solution)/shard_map/all_to_all | solution.py:503
  13.3 2.0 %border_rows.1 = (bf16[24,512]{1,0:T(8,128)(2,1)}, bf16[24,512]{1,0:T(8,128)(2,1)}, bf16[24,512]{1,0:T(8,128)(2,1)}, bf16[24,512]{1,0:T(8,128)(2,1)}) custom-call(bf16[384,512]{1,0:T(8,128)(2,1)} %bitcast.22, s32[4,24]{1,0:T(4,128)} %bitcast.26), custom_call_target="tpu_custom_call" | custom-call | flops 8589934592 | bytes 8388608 | tf_op jit(solution)/shard_map/border_rows/pallas_call | solution.py:101
  15.3 1.1 collective-permute-start
  16.4 4.3 %collective-permute-start.1 = (bf16[24,512]{1,0:T(8,128)(2,1)}, bf16[24,512]{1,0:T(8,128)(2,1)S(1)}, u32[]{:S(2)}, u32[]{:S(2)}) collective-permute-start(bf16[24,512]{1,0:T(8,128)(2,1)} %get-tuple-element.46), channel_id=1, source_target_pairs={{0,15},{1,0},{2,1},{3,2},{4,3},{5,4},{6,5},{7,6},{8,7},{9,8},{10,9... | collective-permute-start | bytes 73736 | tf_op jit(solution)/shard_map/ppermute | solution.py:471
  20.6 1.6 %collective-permute-start.2 = (bf16[24,512]{1,0:T(8,128)(2,1)}, bf16[24,512]{1,0:T(8,128)(2,1)S(1)}, u32[]{:S(2)}, u32[]{:S(2)}) collective-permute-start(bf16[24,512]{1,0:T(8,128)(2,1)} %get-tuple-element.47), channel_id=1, source_target_pairs={{0,16},{16,32},{32,48},{48,64},{64,80},{80,96},{96,112},{1,17},{17... | collective-permute-start | bytes 73736 | tf_op jit(solution)/shard_map/ppermute | solution.py:477
  22.2 1.3 %collective-permute-start.3 = (bf16[24,512]{1,0:T(8,128)(2,1)}, bf16[24,512]{1,0:T(8,128)(2,1)S(1)}, u32[]{:S(2)}, u32[]{:S(2)}) collective-permute-start(bf16[24,512]{1,0:T(8,128)(2,1)} %get-tuple-element.48), channel_id=1, source_target_pairs={{16,0},{32,16},{48,32},{64,48},{80,64},{96,80},{112,96},{17,1},{33... | collective-permute-start | bytes 73736 | tf_op jit(solution)/shard_map/ppermute | solution.py:477
  24.2 0.6 pad_add_fusion.place_ref.count_ref
  24.8 2.0 %collective-permute-done.3.from_south_ref = bf16[24,512]{1,0:T(8,128)(2,1)S(1)} collective-permute-done((bf16[24,512]{1,0:T(8,128)(2,1)}, bf16[24,512]{1,0:T(8,128)(2,1)S(1)}, u32[]{:S(2)}, u32[]{:S(2)}) %collective-permute-start.3) | collective-permute-done | bytes 24608 | tf_op jit(solution)/shard_map/ppermute | solution.py:477
  26.8 0.6 copy-done.10
  27.5 38.6 %mesh_layer.1 = (bf16[384,512]{1,0:T(8,128)(2,1)}, bf16[3072,512]{1,0:T(8,128)(2,1)}, bf16[3072,512]{1,0:T(8,128)(2,1)}, bf16[384,512]{1,0:T(8,128)(2,1)}, f32[3...) custom-call(s32[2]{0:T(128)} %pad_add_fusion.place_ref.count_ref, ...), custom_call_target="tpu_custom_call" | custom-call | flops 19327352832 | bytes 31457280 | tf_op jit(solution)/shard_map/mesh_layer/pallas_call | solution.py:332
  66.1 2.8 %collective-permute-start.4 = (bf16[16,128,512]{2,1,0:T(8,128)(2,1)}, bf16[16,128,512]{2,1,0:T(8,128)(2,1)S(1)}, u32[]{:S(2)}, u32[]{:S(2)}) collective-permute-start(bf16[16,128,512]{2,1,0:T(8,128)(2,1)} %get-tuple-element.52), channel_id=1, source_target_pairs={{0,16},{16,0},{1,17},{17,1},{2,18},{18,2},{3,19},{19,3},{4,20},{20... | collective-permute-start | bytes 6291464 | tf_op jit(solution)/shard_map/ppermute | solution.py:533
  68.8 4.0 %collective-permute-done.4 = bf16[16,128,512]{2,1,0:T(8,128)(2,1)S(1)} collective-permute-done((bf16[16,128,512]{2,1,0:T(8,128)(2,1)}, bf16[16,128,512]{2,1,0:T(8,128)(2,1)S(1)}, u32[]{:S(2)}, u32[]{:S(2)}) %collective-permute-start.4) | collective-permute-done | bytes 2097184 | tf_op jit(solution)/shard_map/ppermute | solution.py:533
  72.8 3.6 %add_convert_fusion = bf16[16,128,512]{2,1,0:T(8,128)(2,1)} fusion(bf16[16,128,512]{2,1,0:T(8,128)(2,1)S(1)} %collective-permute-done.4, bf16[16,128,512]{2,1,0:T(8,128)(2,1)} %get-tuple-element.51), kind=kLoop, calls=%fused_computation.1 | loop fusion | flops 4194304 | bytes 6291456 | tf_op jit(solution)/shard_map/convert_element_type | solution.py:534
  76.5 6.9 %all-to-all-start.1 = ((bf16[64,32,512]{2,1,0:T(8,128)(2,1)}), bf16[64,32,512]{2,1,0:T(8,128)(2,1)S(1)}, u32[]{:S(2)}, u32[]{:S(2)}) async-start(bf16[64,32,512]{2,1,0:T(8,128)(2,1)} %bitcast.13), calls=%async_computation.1 | async-start | bytes 4194304 | tf_op jit(solution)/shard_map/all_to_all | solution.py:536
  83.5 4.9 %collective-permute-start.5 = (bf16[24,512]{1,0:T(8,128)(2,1)S(1)}, bf16[24,512]{1,0:T(8,128)(2,1)S(1)}, u32[]{:S(2)}, u32[]{:S(2)}) collective-permute-start(bf16[24,512]{1,0:T(8,128)(2,1)S(1)} %copy-done.6), channel_id=1, source_target_pairs={{0,15},{1,0},{2,1},{3,2},{4,3},{5,4},{6,5},{7,6},{8,7},{9,8},{10,9... | collective-permute-start | bytes 73736 | tf_op jit(solution)/shard_map/ppermute | solution.py:471
  88.4 1.3 %collective-permute-start.7 = (bf16[24,512]{1,0:T(8,128)(2,1)S(1)}, bf16[24,512]{1,0:T(8,128)(2,1)S(1)}, u32[]{:S(2)}, u32[]{:S(2)}) collective-permute-start(bf16[24,512]{1,0:T(8,128)(2,1)S(1)} %copy-done.4), channel_id=1, source_target_pairs={{16,0},{32,16},{48,32},{64,48},{80,64},{96,80},{112,96},{17,1},{33... | collective-permute-start | bytes 73736 | tf_op jit(solution)/shard_map/ppermute | solution.py:477
  89.7 3.0 %collective-permute-start.8 = (bf16[24,512]{1,0:T(8,128)(2,1)S(1)}, bf16[24,512]{1,0:T(8,128)(2,1)S(1)}, u32[]{:S(2)}, u32[]{:S(2)}) collective-permute-start(bf16[24,512]{1,0:T(8,128)(2,1)S(1)} %copy-done.3), channel_id=1, source_target_pairs={{0,16},{16,32},{32,48},{48,64},{64,80},{80,96},{96,112},{1,17},{17... | collective-permute-start | bytes 73736 | tf_op jit(solution)/shard_map/ppermute | solution.py:477
  92.7 8.4 %edge_grads.1 = f32[3072,512]{1,0:T(8,128)} custom-call(s32[2]{0:T(128)} %pad_add_fusion.place_ref.count_ref, s32[4,1,768]{2,1,0:T(1,128)} %bitcast.25, bf16[3072,512]{1,0:T(8,128)(2,1)} %bitcast.20, bf16[3072,512]{1,0:T(8,128)(2,1)} %get-tuple-element.59.gz_ref, bf16[384,512]{1,0:T(8,128)(2,1)} %get-tuple-element.60.gagg_ref, bf16[1536,512]{1,0:T(8,128)(2,1)} %ew1_ref.3), custom_call_target="tpu_custom_call" | custom-call | flops 2818572288 | bytes 13631488 | tf_op jit(solution)/shard_map/edge_grads/pallas_call | solution.py:411
  101.2 3.1 %collective-permute-done.6 = bf16[24,512]{1,0:T(8,128)(2,1)S(1)} collective-permute-done((bf16[24,512]{1,0:T(8,128)(2,1)S(1)}, bf16[24,512]{1,0:T(8,128)(2,1)S(1)}, u32[]{:S(2)}, u32[]{:S(2)}) %collective-permute-start.6) | collective-permute-done | bytes 24608 | tf_op jit(solution)/shard_map/ppermute | solution.py:471
  104.6 1.0 add.19.node_ref
  105.6 7.8 %all-to-all-done.1 = bf16[64,32,512]{2,1,0:T(8,128)(2,1)S(1)} async-done(((bf16[64,32,512]{2,1,0:T(8,128)(2,1)}), bf16[64,32,512]{2,1,0:T(8,128)(2,1)S(1)}, u32[]{:S(2)}, u32[]{:S(2)}) %all-to-all-start.1) | async-done | bytes 2097184 | tf_op jit(solution)/shard_map/all_to_all | solution.py:536
  113.5 0.9 convert_reduce_fusion.total_ref
  114.4 1.5 %finish_grads.1 = (f32[384,512]{1,0:T(8,128)}, f32[12,512]{1,0:T(8,128)}, f32[4]{0:T(128)}, f32[4,512]{1,0:T(4,128)}, f32[4]{0:T(128)}, /*index=5*/f32[8,512]{1,...) custom-call(s32[1]{0:T(128)} %bitcast.12.lane_ref, ...), custom_call_target="tpu_custom_call", output_to_operand_aliasing={{0}: (2, {})} | custom-call | tf_op jit(solution)/shard_map/finish_grads/pallas_call | solution.py:453
  (31 shorter events, 0.5 us)
Async XLA Ops:
  2.1 24.6 %all-to-all-start = ((bf16[128,2,512]{2,1,0:T(2,128)(2,1)}), bf16[128,2,512]{2,1,0:T(2,128)(2,1)S(1)}, u32[]{:S(2)}, u32[]{:S(2)}) async-start(bf16[128,2,512]{2,1,0:T(2,128)(2,1)} %spread_coarse.1), calls=%async_computation | async-start | bytes 524288 | tf_op jit(solution)/shard_map/all_to_all | solution.py:503
  15.3 9.5 %collective-permute-start = (bf16[24,512]{1,0:T(8,128)(2,1)}, bf16[24,512]{1,0:T(8,128)(2,1)S(1)}, u32[]{:S(2)}, u32[]{:S(2)}) collective-permute-start(bf16[24,512]{1,0:T(8,128)(2,1)} %get-tuple-element.45), channel_id=1, source_target_pairs={{0,1},{1,2},{2,3},{3,4},{4,5},{5,6},{6,7},{7,8},{8,9},{9,10},{10,1... | collective-permute-start | bytes 73736 | tf_op jit(solution)/shard_map/ppermute | solution.py:471
  16.4 8.4 %collective-permute-start.1 = (bf16[24,512]{1,0:T(8,128)(2,1)}, bf16[24,512]{1,0:T(8,128)(2,1)S(1)}, u32[]{:S(2)}, u32[]{:S(2)}) collective-permute-start(bf16[24,512]{1,0:T(8,128)(2,1)} %get-tuple-element.46), channel_id=1, source_target_pairs={{0,15},{1,0},{2,1},{3,2},{4,3},{5,4},{6,5},{7,6},{8,7},{9,8},{10,9... | collective-permute-start | bytes 73736 | tf_op jit(solution)/shard_map/ppermute | solution.py:471
  20.6 4.1 %collective-permute-start.2 = (bf16[24,512]{1,0:T(8,128)(2,1)}, bf16[24,512]{1,0:T(8,128)(2,1)S(1)}, u32[]{:S(2)}, u32[]{:S(2)}) collective-permute-start(bf16[24,512]{1,0:T(8,128)(2,1)} %get-tuple-element.47), channel_id=1, source_target_pairs={{0,16},{16,32},{32,48},{48,64},{64,80},{80,96},{96,112},{1,17},{17... | collective-permute-start | bytes 73736 | tf_op jit(solution)/shard_map/ppermute | solution.py:477
  22.2 4.5 %collective-permute-start.3 = (bf16[24,512]{1,0:T(8,128)(2,1)}, bf16[24,512]{1,0:T(8,128)(2,1)S(1)}, u32[]{:S(2)}, u32[]{:S(2)}) collective-permute-start(bf16[24,512]{1,0:T(8,128)(2,1)} %get-tuple-element.48), channel_id=1, source_target_pairs={{16,0},{32,16},{48,32},{64,48},{80,64},{96,80},{112,96},{17,1},{33... | collective-permute-start | bytes 73736 | tf_op jit(solution)/shard_map/ppermute | solution.py:477
  24.8 2.0 %copy-start.7 = (bf16[24,512]{1,0:T(8,128)(2,1)}, bf16[24,512]{1,0:T(8,128)(2,1)S(1)}, u32[]{:S(2)}) copy-start(bf16[24,512]{1,0:T(8,128)(2,1)S(1)} %collective-permute-done.from_east_ref) | copy-start | bytes 73732
  24.8 2.0 %copy-start.8 = (bf16[24,512]{1,0:T(8,128)(2,1)}, bf16[24,512]{1,0:T(8,128)(2,1)S(1)}, u32[]{:S(2)}) copy-start(bf16[24,512]{1,0:T(8,128)(2,1)S(1)} %collective-permute-done.1.from_west_ref) | copy-start | bytes 73732
  24.8 2.0 %copy-start.9 = (bf16[24,512]{1,0:T(8,128)(2,1)}, bf16[24,512]{1,0:T(8,128)(2,1)S(1)}, u32[]{:S(2)}) copy-start(bf16[24,512]{1,0:T(8,128)(2,1)S(1)} %collective-permute-done.2.from_north_ref) | copy-start | bytes 73732
  26.7 0.6 copy-start.10
  26.8 0.7 copy-start.1
  66.1 6.8 %collective-permute-start.4 = (bf16[16,128,512]{2,1,0:T(8,128)(2,1)}, bf16[16,128,512]{2,1,0:T(8,128)(2,1)S(1)}, u32[]{:S(2)}, u32[]{:S(2)}) collective-permute-start(bf16[16,128,512]{2,1,0:T(8,128)(2,1)} %get-tuple-element.52), channel_id=1, source_target_pairs={{0,16},{16,0},{1,17},{17,1},{2,18},{18,2},{3,19},{19,3},{4,20},{20... | collective-permute-start | bytes 6291464 | tf_op jit(solution)/shard_map/ppermute | solution.py:533
  76.5 6.9 %copy-start.2 = (s32[1,1,4,24]{3,2,1,0:T(4,128)S(1)}, s32[1,1,4,24]{3,2,1,0:T(4,128)}, u32[]{:S(2)}) copy-start(s32[1,1,4,24]{3,2,1,0:T(4,128)} %param.22) | copy-start | bytes 1156
  76.5 7.0 %copy-start.6 = (bf16[24,512]{1,0:T(8,128)(2,1)S(1)}, bf16[24,512]{1,0:T(8,128)(2,1)}, u32[]{:S(2)}) copy-start(bf16[24,512]{1,0:T(8,128)(2,1)} %get-tuple-element.62) | copy-start | bytes 73732
  76.5 11.9 %copy-start.5 = (bf16[24,512]{1,0:T(8,128)(2,1)S(1)}, bf16[24,512]{1,0:T(8,128)(2,1)}, u32[]{:S(2)}) copy-start(bf16[24,512]{1,0:T(8,128)(2,1)} %get-tuple-element.63) | copy-start | bytes 73732
  76.5 11.9 %copy-start.4 = (bf16[24,512]{1,0:T(8,128)(2,1)S(1)}, bf16[24,512]{1,0:T(8,128)(2,1)}, u32[]{:S(2)}) copy-start(bf16[24,512]{1,0:T(8,128)(2,1)} %get-tuple-element.64) | copy-start | bytes 73732
  76.5 13.2 %copy-start.3 = (bf16[24,512]{1,0:T(8,128)(2,1)S(1)}, bf16[24,512]{1,0:T(8,128)(2,1)}, u32[]{:S(2)}) copy-start(bf16[24,512]{1,0:T(8,128)(2,1)} %get-tuple-element.65) | copy-start | bytes 73732
  76.5 37.0 %all-to-all-start.1 = ((bf16[64,32,512]{2,1,0:T(8,128)(2,1)}), bf16[64,32,512]{2,1,0:T(8,128)(2,1)S(1)}, u32[]{:S(2)}, u32[]{:S(2)}) async-start(bf16[64,32,512]{2,1,0:T(8,128)(2,1)} %bitcast.13), calls=%async_computation.1 | async-start | bytes 4194304 | tf_op jit(solution)/shard_map/all_to_all | solution.py:536
  83.5 17.7 %collective-permute-start.5 = (bf16[24,512]{1,0:T(8,128)(2,1)S(1)}, bf16[24,512]{1,0:T(8,128)(2,1)S(1)}, u32[]{:S(2)}, u32[]{:S(2)}) collective-permute-start(bf16[24,512]{1,0:T(8,128)(2,1)S(1)} %copy-done.6), channel_id=1, source_target_pairs={{0,15},{1,0},{2,1},{3,2},{4,3},{5,4},{6,5},{7,6},{8,7},{9,8},{10,9... | collective-permute-start | bytes 73736 | tf_op jit(solution)/shard_map/ppermute | solution.py:471
  88.4 15.9 %collective-permute-start.6 = (bf16[24,512]{1,0:T(8,128)(2,1)S(1)}, bf16[24,512]{1,0:T(8,128)(2,1)S(1)}, u32[]{:S(2)}, u32[]{:S(2)}) collective-permute-start(bf16[24,512]{1,0:T(8,128)(2,1)S(1)} %copy-done.5), channel_id=1, source_target_pairs={{0,1},{1,2},{2,3},{3,4},{4,5},{5,6},{6,7},{7,8},{8,9},{9,10},{10,1... | collective-permute-start | bytes 73736 | tf_op jit(solution)/shard_map/ppermute | solution.py:471
  88.4 15.9 %collective-permute-start.7 = (bf16[24,512]{1,0:T(8,128)(2,1)S(1)}, bf16[24,512]{1,0:T(8,128)(2,1)S(1)}, u32[]{:S(2)}, u32[]{:S(2)}) collective-permute-start(bf16[24,512]{1,0:T(8,128)(2,1)S(1)} %copy-done.4), channel_id=1, source_target_pairs={{16,0},{32,16},{48,32},{64,48},{80,64},{96,80},{112,96},{17,1},{33... | collective-permute-start | bytes 73736 | tf_op jit(solution)/shard_map/ppermute | solution.py:477
  89.7 14.6 %collective-permute-start.8 = (bf16[24,512]{1,0:T(8,128)(2,1)S(1)}, bf16[24,512]{1,0:T(8,128)(2,1)S(1)}, u32[]{:S(2)}, u32[]{:S(2)}) collective-permute-start(bf16[24,512]{1,0:T(8,128)(2,1)S(1)} %copy-done.3), channel_id=1, source_target_pairs={{0,16},{16,32},{32,48},{48,64},{64,80},{80,96},{96,112},{1,17},{17... | collective-permute-start | bytes 73736 | tf_op jit(solution)/shard_map/ppermute | solution.py:477
  92.7 11.9 %copy-start = (f32[384,512]{1,0:T(8,128)S(1)}, f32[384,512]{1,0:T(8,128)}, u32[]{:S(2)}) copy-start(f32[384,512]{1,0:T(8,128)} %get-tuple-element.61) | copy-start | bytes 2359300
where the time goes:
time: 117 us; the launch traced here: 116 us
  Pallas kernels  52 us (44%)
  starting transfers between devices  38.2 us (33%)
  waiting for transfers between devices  16.9 us (14%)
  other arithmetic  6.17 us (5%)
  between operations  1.47 us (1%)
    pallas_call x1, Pallas kernels, layer(): pl.pallas_call(layer_kernel, name='mesh_layer', grid=(2 * STEPS,), in_spe...  38.6 us
    all_to_all x1, starting transfers between devices, shards(): lax.all_to_all(spread(nodes_l), LAT_LON, split_axis=0, concat_axis=0, til...  11.1 us
    ppermute x4, starting transfers between devices, ring(): lax.ppermute(block, axis, [(i, (i + distance) % n) for i in range(n)])  10.3 us
    pallas_call x1, Pallas kernels, edge_grads(): pl.pallas_call(edge_grad_kernel, name='edge_grads', grid=(STEPS,), in_spe...  8.45 us
    all_to_all x1, waiting for transfers between devices, shards(): lax.all_to_all(both, ('lat_0', 'lon_0', 'lon_1'), split_axis=0, concat_ax...  7.84 us
    ppermute x4, starting transfers between devices, passed_along(): lax.ppermute(value, axis, [(source, source + steps) for source in range(l...  7.18 us
    all_to_all x1, starting transfers between devices, shards(): lax.all_to_all(both, ('lat_0', 'lon_0', 'lon_1'), split_axis=0, concat_ax...  6.86 us
    ppermute x1, waiting for transfers between devices, shards(): pair = lax.ppermute(send, 'lat_1', [(0, 1), (1, 0)])  4 us
  transfers between devices with their start and end apart: 11, of which 4 were waited for; matrix products, arithmetic and copies ran while one was open for 2% of the time, Pallas kernels for 9%

commit v1 on v0

v1 whole, which is shorter than its diff:
```python
import functools

import jax
import jax.numpy as jnp
from jax import lax
from jax.experimental import pallas as pl
from jax.experimental.pallas import tpu as pltpu
from jax.sharding import Mesh
from jax.sharding import PartitionSpec as P

COARSE = 2
LON = ("lon_0", "lon_1")
LAT = ("lat_0", "lat_1")
LAT_LON = ("lat_0", "lat_1", "lon_0", "lon_1")
EPS = 1e-05
BF = jnp.bfloat16
F32 = jnp.float32

NODES = 384
HALO = 24
WIDE = 512
EDGES = 3072
FAR = 128
BLOCK = 1024
STEPS = EDGES // BLOCK
SENDERS = 640
ONES_ROW = 608
TABLE = SENDERS + NODES
FIRST = WIDE + SENDERS
GROUPS = 32
GROUP_ROWS = 128


def mm(a, b):
    return lax.dot_general(a, b, (((1,), (0,)), ((), ())), preferred_element_type=F32)


def mm_t(a, b):
    return lax.dot_general(a, b, (((1,), (1,)), ((), ())), preferred_element_type=F32)


def t_mm(a, b):
    return lax.dot_general(a, b, (((0,), (0,)), ((), ())), preferred_element_type=F32)


def row_mean(v):
    return jnp.sum(v, axis=1, keepdims=True) * (1.0 / WIDE)


def first_act(z):
    sig = 0.5 + 0.5 * jnp.tanh(0.5 * z)
    act = z * sig
    return act, sig + act * (1.0 - sig)


def normalise(z):
    centred = z - row_mean(z)
    rstd = lax.rsqrt(row_mean(centred * centred) + EPS)
    return centred * rstd, rstd


def norm_back(g, normed, rstd, gain):
    s = g * gain
    return rstd * (s - row_mean(s) - normed * row_mean(s * normed))


def lane_ids(row):
    return jnp.transpose(jnp.broadcast_to(row, (128, BLOCK)))


def hot_lanes(ids, first, chunks):
    lane = lax.broadcasted_iota(jnp.int32, (BLOCK, 128), 1).astype(F32)
    return [
        jnp.where(ids == lane + float(first + 128 * j), 1.0, 0.0).astype(BF) for j in range(chunks)
    ]


def spread_kernel(nodes_ref, coarse_ref):
    coarse_ref[...] = jnp.broadcast_to(nodes_ref[0:COARSE][None], (FAR, COARSE, WIDE))


def spread(nodes):
    return pl.pallas_call(
        spread_kernel,
        name="spread_coarse",
        grid=(1,),
        in_specs=[pl.BlockSpec((16, WIDE), lambda i: (0, 0))],
        out_specs=pl.BlockSpec((FAR, COARSE, WIDE), lambda i: (0, 0, 0)),
        out_shape=jax.ShapeDtypeStruct((FAR, COARSE, WIDE), BF),
    )(nodes)


def border_kernel(place_ref, nodes_ref, rows_ref, *sent_refs):
    at = lax.broadcasted_iota(jnp.int32, (NODES, HALO), 0)
    for k, sent_ref in enumerate(sent_refs):
        first = 2 * (k // 2)
        odd = place_ref[2 - k // 2] != 0
        one, two = rows_ref[first + k % 2], rows_ref[first + 1 - k % 2]
        hot = jnp.where(at == jnp.where(odd, two, one).reshape(1, HALO), 1.0, 0.0).astype(BF)
        sent_ref[...] = t_mm(hot, nodes_ref[...]).astype(BF)


def borders(place, nodes, rows_out):
    vmem = pl.BlockSpec(memory_space=pltpu.VMEM)
    return pl.pallas_call(
        border_kernel,
        name="border_rows",
        in_specs=[pl.BlockSpec(memory_space=pltpu.SMEM), vmem, vmem],
        out_shape=[jax.ShapeDtypeStruct((HALO, WIDE), BF)] * 4,
        cost_estimate=pl.CostEstimate(
            flops=8 << 30, transcendentals=0, bytes_accessed=8 << 20
        ),
    )(place, nodes, rows_out)


def whole(*shape):
    return pl.BlockSpec(shape, lambda i: (0,) * len(shape), pipeline_mode=pl.Buffered(1))


def by_block(shape, pick):
    return pl.BlockSpec(shape, lambda i: (pick(i),) + (0,) * (len(shape) - 1))


def params():
    return pltpu.CompilerParams(
        dimension_semantics=("arbitrary",), vmem_limit_bytes=60 * 1024 * 1024
    )


def layer_kernel(
    place_ref,
    snd_ref,
    rcv_ref,
    need_ref,
    lon_a_ref,
    lon_b_ref,
    lat_a_ref,
    lat_b_ref,
    far_ref,
    eb1_ref,
    eg_ref,
    nb1_ref,
    ng_ref,
    edges_hbm,
    ecot_hbm,
    nodes_hbm,
    ncot_hbm,
    ew1_hbm,
    ew2_hbm,
    nw1_hbm,
    nw2_hbm,
    east_ref,
    west_ref,
    north_ref,
    south_ref,
    new_nodes_hbm,
    new_edges_hbm,
    gz_hbm,
    gagg_hbm,
    node_hbm,
    keep_hbm,
    send_hbm,
    nodes_ref,
    ncot_ref,
    ew1_ref,
    ew2_ref,
    nw1_ref,
    nw2_ref,
    table_s,
    right_s,
    left_s,
    ecot_s,
    fresh_s,
    act_s,
    dact_s,
    normed_s,
    rstd_s,
    new_nodes_s,
    gagg_s,
    node_s,
    agg_s,
    dw1_s,
    dw2_s,
    gain_s,
    packed_s,
    whole_sem,
    edges_sem,
    ecot_sem,
    fresh_sem,
    gz_sem,
    packed_sem,
):
    count = place_ref[0]
    egain = eg_ref[...].reshape(1, WIDE)

    def rows_of(i):
        return pl.ds(pl.multiple_of(i * BLOCK, BLOCK), BLOCK)

    def fetch(k):
        pairs = (
            (nodes_hbm, nodes_ref),
            (ew1_hbm, ew1_ref),
            (ew2_hbm, ew2_ref),
            (nw1_hbm, nw1_ref),
            (nw2_hbm, nw2_ref),
            (ncot_hbm, ncot_ref),
        )
        return pltpu.make_async_copy(*pairs[k], whole_sem.at[k])

    def give(k):
        pairs = ((new_nodes_s, new_nodes_hbm), (gagg_s, gagg_hbm), (node_s, node_hbm))
        return pltpu.make_async_copy(*pairs[k], whole_sem.at[6 + k])

    def edges_in(i):
        here = rows_of(i)
        return pltpu.make_async_copy(edges_hbm.at[here], left_s.at[here, 0:WIDE], edges_sem.at[i])

    def ecot_in(i):
        here = rows_of(i)
        return pltpu.make_async_copy(ecot_hbm.at[here], ecot_s.at[here], ecot_sem.at[i])

    def fresh_out(i):
        here = rows_of(i)
        return pltpu.make_async_copy(fresh_s.at[here], new_edges_hbm.at[here], fresh_sem.at[i])

    def gz_out(i):
        here = rows_of(i)
        return pltpu.make_async_copy(ecot_s.at[here], gz_hbm.at[here], gz_sem.at[i])

    def packed_out(g):
        copies = []
        for other, ref in ((0, keep_hbm), (1, send_hbm)):
            group = (g >> 2) * 8 + (place_ref[1] ^ other) * 4 + (g & 3)
            copies.append(
                pltpu.make_async_copy(packed_s.at[group], ref.at[g], packed_sem.at[2 * g + other])
            )
        return copies

    fetch(0).start()
    fetch(1).start()
    edges_in(0).start()
    fetch(2).start()
    for i in range(1, STEPS):
        edges_in(i).start()
    for k in range(3, 6):
        fetch(k).start()
    for i in range(STEPS):
        ecot_in(i).start()

    agg_s[...] = jnp.zeros_like(agg_s)
    dw1_s[...] = jnp.zeros_like(dw1_s)
    dw2_s[...] = jnp.zeros_like(dw2_s)
    gain_s[...] = jnp.zeros_like(gain_s)
    odd_lat, odd_lon = place_ref[1] != 0, place_ref[2] != 0
    lon_a, lon_b, lat_a, lat_b = (
        ref[...].astype(F32) for ref in (lon_a_ref, lon_b_ref, lat_a_ref, lat_b_ref)
    )
    table_s[NODES : NODES + 96] = jnp.concatenate(
        [
            jnp.where(odd_lon, lon_a, lon_b),
            jnp.where(odd_lon, lon_b, lon_a),
            jnp.where(odd_lat, lat_a, lat_b),
            jnp.where(odd_lat, lat_b, lat_a),
        ],
        axis=0,
    ).astype(BF)
    pick = jnp.transpose(jnp.broadcast_to(need_ref[...].astype(F32), (128, 128)))[:, 0:1]
    low, high = far_ref[:, 0].astype(F32), far_ref[:, 1].astype(F32)
    table_s[480:608] = jnp.where(pick == 0.0, low, high).astype(BF)
    table_s[608:SENDERS] = jnp.zeros((32, WIDE), BF)
    fetch(0).wait()
    table_s[0:NODES] = nodes_ref[...]
    fetch(1).wait()
    right_s[0:WIDE] = ew1_ref[0:WIDE]
    right_s[WIDE:FIRST] = mm(table_s[...], ew1_ref[WIDE : 2 * WIDE]).astype(BF)
    right_s[FIRST:] = mm(nodes_ref[...], ew1_ref[2 * WIDE :]).astype(BF)
    fetch(2).wait()

    def forward(i, carry):
        here = rows_of(i)
        at = i * BLOCK
        slot = lax.broadcasted_iota(jnp.int32, (1, BLOCK), 1) + at
        snd = snd_ref[i].astype(F32)
        rcv = jnp.where(slot < count, rcv_ref[i].astype(F32), -1.0)
        hots = hot_lanes(lane_ids(snd), 0, SENDERS // 128)
        lane = lax.broadcasted_iota(jnp.int32, (BLOCK, 128), 1)
        hots[4] = jnp.where(lane == ONES_ROW - 512, 1.0, hots[4].astype(F32)).astype(BF)
        hots += hot_lanes(lane_ids(rcv), 0, NODES // 128)
        for k, hot in enumerate(hots):
            left_s[here, WIDE + 128 * k : WIDE + 128 * (k + 1)] = hot
        edges_in(i).wait()
        z1 = mm(left_s[here], right_s[...]) + eb1_ref[...].reshape(1, WIDE)
        act, dact = first_act(z1)
        act = act.astype(BF)
        act_s[here] = act
        dact_s[here] = dact.astype(BF)
        normed, rstd = normalise(mm(act, ew2_ref[...]))
        normed_s[here] = normed.astype(BF)
        rstd_s[here] = jnp.broadcast_to(rstd, (BLOCK, 128))
        live = (lax.broadcasted_iota(jnp.int32, (BLOCK, 1), 0) + at < count).astype(F32)
        fresh = (left_s[here, 0:WIDE].astype(F32) + (live * normed) * egain).astype(BF)
        fresh_s[here] = fresh
        fresh_out(i).start()
        agg_s[...] += t_mm(left_s[here, FIRST:], fresh)
        return carry

    lax.fori_loop(0, STEPS, forward, 0)

    for k in range(3, 6):
        fetch(k).wait()
    nodes = nodes_ref[...]
    ngain = ng_ref[...].reshape(1, WIDE)
    agg = agg_s[...].astype(BF)
    z1 = mm(nodes, nw1_ref[0:WIDE]) + mm(agg, nw1_ref[WIDE:]) + nb1_ref[...].reshape(1, WIDE)
    act, dact = first_act(z1)
    act = act.astype(BF)
    normed, rstd = normalise(mm(act, nw2_ref[...]))
    new_nodes_s[...] = (nodes.astype(F32) + normed * ngain).astype(BF)
    give(0).start()
    cot = ncot_ref[...].astype(F32)
    gz2 = norm_back(cot, normed, rstd, ngain).astype(BF)
    gain_grad = jnp.sum(cot * normed, axis=0, keepdims=True)
    gz1 = (mm_t(gz2, nw2_ref[...]) * dact).astype(BF)
    bias_grad = jnp.sum(gz1.astype(F32), axis=0, keepdims=True)
    gagg_s[...] = mm_t(gz1, nw1_ref[WIDE:]).astype(BF)
    give(1).start()
    node_s[...] = cot + mm_t(gz1, nw1_ref[0:WIDE])
    packed_s[0:16, 0:32] = t_mm(nodes, gz1).astype(BF).reshape(16, 32, WIDE)
    packed_s[16:32, 0:32] = t_mm(agg, gz1).astype(BF).reshape(16, 32, WIDE)
    packed_s[:, 32:48] = t_mm(act, gz2).astype(BF).reshape(GROUPS, 16, WIDE)

    def backward(i, carry):
        here = rows_of(i)
        live = (lax.broadcasted_iota(jnp.int32, (BLOCK, 1), 0) + i * BLOCK < count).astype(F32)
        ecot_in(i).wait()
        g = live * ecot_s[here].astype(F32) + mm(left_s[here, FIRST:], gagg_s[...])
        normed = normed_s[here].astype(F32)
        gain_s[...] += jnp.sum((g * normed).reshape(BLOCK // 8, 8, WIDE), axis=0)
        gz2 = norm_back(g, normed, rstd_s[here][:, 0:1], egain).astype(BF)
        dw2_s[...] += t_mm(act_s[here], gz2)
        gz1 = (mm_t(gz2, ew2_ref[...]) * dact_s[here].astype(F32)).astype(BF)
        ecot_s[here] = gz1
        gz_out(i).start()
        dw1_s[...] += t_mm(left_s[here], gz1)
        return carry

    lax.fori_loop(0, STEPS, backward, 0)

    sent, got = dw1_s[WIDE:FIRST].astype(BF), dw1_s[FIRST:].astype(BF)
    back = mm_t(sent, ew1_ref[WIDE : 2 * WIDE])
    node_s[...] += back[0:NODES] + mm_t(got, ew1_ref[2 * WIDE :])
    give(2).start()
    packed_s[:, 96:112] = dw2_s[...].astype(BF).reshape(GROUPS, 16, WIDE)
    first = jnp.concatenate(
        [
            dw1_s[0:WIDE].astype(BF),
            t_mm(table_s[...], sent).astype(BF),
            t_mm(nodes, got).astype(BF),
        ],
        axis=0,
    )
    packed_s[:, 48:96] = first.reshape(GROUPS, 48, WIDE)
    for k, ref in enumerate((east_ref, west_ref, north_ref, south_ref)):
        ref[...] = back[NODES + HALO * k : NODES + HALO * (k + 1)].astype(BF)
    vectors = (
        dw1_s[WIDE + ONES_ROW : WIDE + ONES_ROW + 1],
        jnp.sum(gain_s[...], axis=0, keepdims=True),
        bias_grad,
        gain_grad,
    )
    half = WIDE // 2
    paired = [
        jnp.concatenate([vectors[k][:, side], vectors[k + 1][:, side]], axis=1)
        for side in (slice(0, half), slice(half, WIDE))
        for k in (0, 2)
    ]
    extra = jnp.concatenate([back[480:608]] + paired + [jnp.zeros((124, WIDE), F32)], axis=0)
    out = lax.broadcasted_iota(jnp.int32, (GROUPS * 16, 256), 0)
    src = lax.broadcasted_iota(jnp.int32, (GROUPS * 16, 256), 1)
    need = jnp.concatenate([need_ref[...], jnp.zeros((1, 128), jnp.int32)], axis=1)
    slot = out & 15
    low = (slot < 4) & (src == (out >> 4) * 4 + slot) & (need == 0)
    high = (slot >= 4) & (slot < 8) & (src == (out >> 4) * 4 + slot - 4) & (need == 1)
    small = (slot >= 8) & (slot < 10) & (src == 120 + slot + (out >> 8) * 2)
    move = jnp.where(low | high | small, 1.0, 0.0).astype(BF)
    packed_s[:, 112:128] = mm(move, extra.astype(BF)).astype(BF).reshape(GROUPS, 16, WIDE)
    out = lax.broadcasted_iota(jnp.int32, (128, 128), 0)
    src = lax.broadcasted_iota(jnp.int32, (128, 128), 1)
    z, slot = out >> 5, out & 31
    want = jnp.where(slot < 8, 8 * z + slot, 24 + 4 * z + slot)
    want = jnp.where(slot >= 12, 36 + 12 * z + slot, want)
    want = jnp.where(slot >= 24, 72 + 4 * z + slot, want)
    want = jnp.where(slot >= 28, 112 + z + 4 * (slot - 28), want)
    want = jnp.where(slot >= 30, 90 + slot, want)
    order = jnp.where(src == want, 1.0, 0.0).astype(BF)
    for g in range(16):
        for group in ((g >> 2) * 8 + (g & 3), (g >> 2) * 8 + 4 + (g & 3)):
            packed_s[group] = mm(order, packed_s[group]).astype(BF)
        for copy in packed_out(g):
            copy.start()
    for k in range(3):
        give(k).wait()
    for i in range(STEPS):
        fresh_out(i).wait()
        gz_out(i).wait()
    for g in range(16):
        for copy in packed_out(g):
            copy.wait()


def layer(place, snd, rcv, need, edges, ecot, nodes, borders, far, ncot, ew1, ew2, nw1, nw2, eb1, eg, nb1, ng):
    sds = jax.ShapeDtypeStruct
    vmem = pl.BlockSpec(memory_space=pltpu.VMEM)
    hbm = pl.BlockSpec(memory_space=pl.ANY)
    return pl.pallas_call(
        layer_kernel,
        name="mesh_layer",
        in_specs=[pl.BlockSpec(memory_space=pltpu.SMEM)] + [vmem] * 12 + [hbm] * 8,
        out_specs=[vmem] * 4 + [hbm] * 7,
        out_shape=[sds((HALO, WIDE), BF)] * 4
        + [
            sds((NODES, WIDE), BF),
            sds((EDGES, WIDE), BF),
            sds((EDGES, WIDE), BF),
            sds((NODES, WIDE), BF),
            sds((NODES, WIDE), F32),
        ]
        + [sds((16, GROUP_ROWS, WIDE), BF)] * 2,
        scratch_shapes=[
            pltpu.VMEM((NODES, WIDE), BF),
            pltpu.VMEM((NODES, WIDE), BF),
            pltpu.VMEM((3 * WIDE, WIDE), BF),
            pltpu.VMEM((WIDE, WIDE), BF),
            pltpu.VMEM((2 * WIDE, WIDE), BF),
            pltpu.VMEM((WIDE, WIDE), BF),
            pltpu.VMEM((SENDERS, WIDE), BF),
            pltpu.VMEM((WIDE + TABLE, WIDE), BF),
            pltpu.VMEM((EDGES, WIDE + TABLE), BF),
            pltpu.VMEM((EDGES, WIDE), BF),
            pltpu.VMEM((EDGES, WIDE), BF),
            pltpu.VMEM((EDGES, WIDE), BF),
            pltpu.VMEM((EDGES, WIDE), BF),
            pltpu.VMEM((EDGES, WIDE), BF),
            pltpu.VMEM((EDGES, 128), F32),
            pltpu.VMEM((NODES, WIDE), BF),
            pltpu.VMEM((NODES, WIDE), BF),
            pltpu.VMEM((NODES, WIDE), F32),
            pltpu.VMEM((NODES, WIDE), F32),
            pltpu.VMEM((WIDE + TABLE, WIDE), F32),
            pltpu.VMEM((WIDE, WIDE), F32),
            pltpu.VMEM((8, WIDE), F32),
            pltpu.VMEM((GROUPS, GROUP_ROWS, WIDE), BF),
            pltpu.SemaphoreType.DMA((9,)),
            pltpu.SemaphoreType.DMA((STEPS,)),
            pltpu.SemaphoreType.DMA((STEPS,)),
            pltpu.SemaphoreType.DMA((STEPS,)),
            pltpu.SemaphoreType.DMA((STEPS,)),
            pltpu.SemaphoreType.DMA((32,)),
        ],
        compiler_params=pltpu.CompilerParams(vmem_limit_bytes=60 * 1024 * 1024),
        cost_estimate=pl.CostEstimate(
            flops=18 << 30, transcendentals=4 << 20, bytes_accessed=30 << 20
        ),
    )(place, snd, rcv, need, *borders, far, eb1, eg, nb1, ng, edges, ecot, nodes, ncot, ew1, ew2, nw1, nw2)


def edge_grad_kernel(count_ref, rcv_ref, ecot_ref, gz_ref, gagg_ref, ew1_ref, out_ref):
    at = pl.program_id(0) * BLOCK
    back = jnp.concatenate(hot_lanes(lane_ids(rcv_ref[0].astype(F32)), 0, NODES // 128), axis=1)
    live = (lax.broadcasted_iota(jnp.int32, (BLOCK, 1), 0) + at < count_ref[0]).astype(F32)
    taken = live * mm(back, gagg_ref[...])
    out_ref[...] = ecot_ref[...].astype(F32) + taken + mm_t(gz_ref[...], ew1_ref[...])


def edge_grads(place, rcv, ecot, gz, gagg, ew1):
    same = lambda i: i
    return pl.pallas_call(
        edge_grad_kernel,
        name="edge_grads",
        grid=(STEPS,),
        in_specs=[
            pl.BlockSpec(memory_space=pltpu.SMEM),
            by_block((1, 1, BLOCK), same),
            by_block((BLOCK, WIDE), same),
            by_block((BLOCK, WIDE), same),
            whole(NODES, WIDE),
            whole(WIDE, WIDE),
        ],
        out_specs=by_block((BLOCK, WIDE), same),
        out_shape=jax.ShapeDtypeStruct((EDGES, WIDE), F32),
        compiler_params=params(),
        cost_estimate=pl.CostEstimate(
            flops=2 * EDGES * WIDE * (WIDE + NODES), transcendentals=0, bytes_accessed=13 << 20
        ),
    )(place, rcv, ecot, gz, gagg, ew1)


def finish_kernel(lane_ref, total_ref, node_ref, out_ref, *grads):
    total = total_ref[...]
    ew1, eb1, ew2, eg, nw1, nb1, nw2, ng = grads
    nw1[...] = total[0:8]
    nw2[...] = total[8:12]
    ew1[...] = total[12:24]
    ew2[...] = total[24:28]
    out_ref[...] = node_ref[...]
    out_ref[0:COARSE] += total[28:30]
    half = WIDE // 2
    lines = [total[30:31, :half], total[30:31, half:], total[31:32, :half], total[31:32, half:]]
    lines = jnp.concatenate(lines + [jnp.zeros((4, half), F32)], axis=0)
    lines = pltpu.roll(lines, (half - lane_ref[0]) & (half - 1), 1)
    for k, ref in enumerate((eb1, eg, nb1, ng)):
        ref[...] = lines[k, 0:4]


def finish(lane, total, node_grad):
    sds = jax.ShapeDtypeStruct
    rows = [(12, WIDE), (4,), (4, WIDE), (4,), (8, WIDE), (4,), (4, WIDE), (4,)]
    first = pl.BlockSpec((8, WIDE), lambda i: (0, 0))
    return pl.pallas_call(
        finish_kernel,
        name="finish_grads",
        grid=(1,),
        in_specs=[
            pl.BlockSpec(memory_space=pltpu.SMEM),
            whole(GROUP_ROWS // 4, WIDE),
            first,
        ],
        out_specs=[first] + [pl.BlockSpec(r, lambda i, n=len(r): (0,) * n) for r in rows],
        out_shape=[sds((NODES, WIDE), F32)] + [sds(r, F32) for r in rows],
        input_output_aliases={2: 0},
        compiler_params=params(),
    )(lane, total, node_grad)


def ring(block, axis, distance):
    n = lax.axis_size(axis)
    return lax.ppermute(block, axis, [(i, (i + distance) % n) for i in range(n)])


def swap(block, axis, first, around):
    n = lax.axis_size(axis)
    pairs = [(i, (i + 1) % n) for i in range(first, n, 2) if around or i + 1 < n]
    return lax.ppermute(block, axis, pairs + [(j, i) for i, j in pairs])


def passed_along(value, axis, steps):
    count = lax.axis_size(axis)
    leading, last = (max(0, -steps), min(count, count - steps))
    return lax.ppermute(value, axis, [(source, source + steps) for source in range(leading, last)])


def shards(
    nodes,
    edges,
    senders,
    receivers,
    edge_count,
    halo_send,
    long_need,
    node_cot,
    edge_cot,
    e_w1,
    e_b1,
    e_w2,
    e_gain,
    n_w1,
    n_b1,
    n_w2,
    n_gain,
):
    nodes_l, edges_l, ecot = nodes[0, 0], edges[0, 0], edge_cot[0, 0]
    rows_out = halo_send[0, 0]
    snd = senders.reshape(STEPS, 1, BLOCK)
    rcv = receivers.reshape(STEPS, 1, BLOCK)
    far = lax.all_to_all(spread(nodes_l), LAT_LON, split_axis=0, concat_axis=0, tiled=True)
    place = jnp.stack(
        [
            edge_count[0, 0],
            lax.axis_index("lat_1").astype(jnp.int32),
            (lax.axis_index("lon_1") & 1).astype(jnp.int32),
        ]
    )
    sent = borders(place, nodes_l, rows_out)
    halo = [
        swap(sent[0], LON, 0, True),
        swap(sent[1], LON, 1, True),
        swap(sent[2], LAT, 0, False),
        swap(sent[3], LAT, 1, False),
    ]
    *halo_grad, new_nodes, new_edges, gz, gagg, node_part, keep, send = layer(
        place,
        snd,
        rcv,
        long_need.reshape(1, FAR),
        edges_l,
        ecot,
        nodes_l,
        halo,
        far,
        node_cot[0, 0],
        e_w1,
        e_w2,
        n_w1,
        n_w2,
        e_b1,
        e_gain,
        n_b1,
        n_gain,
    )
    pair = lax.ppermute(send, "lat_1", [(0, 1), (1, 0)])
    both = (keep.astype(F32) + pair.astype(F32)).astype(BF).reshape(64, GROUP_ROWS // 4, WIDE)
    both, halo_grad, gz = lax.optimization_barrier((both, halo_grad, gz))
    parts = lax.all_to_all(
        both, ("lat_0", "lon_0", "lon_1"), split_axis=0, concat_axis=0, tiled=True
    )
    edge_grad = edge_grads(place, rcv, ecot, gz, gagg, e_w1)
    returned = [
        ring(halo_grad[0], LON, -1),
        ring(halo_grad[1], LON, 1),
        passed_along(halo_grad[2], LAT, -1),
        passed_along(halo_grad[3], LAT, 1),
    ]
    border = (rows_out.reshape(1, 4 * HALO) == lax.broadcasted_iota(jnp.int32, (NODES, 4 * HALO), 0)).astype(BF)
    node_grad = node_part + jnp.dot(border, jnp.concatenate(returned, axis=0), preferred_element_type=F32)
    parts, edge_grad, node_grad = lax.optimization_barrier((parts, edge_grad, node_grad))
    lane = ((lax.axis_index(LAT_LON) & 63) * 4).astype(jnp.int32).reshape(1)
    node_grad, *sums = finish(lane, jnp.sum(parts.astype(F32), axis=0), node_grad)
    return (
        new_nodes[None, None],
        new_edges[None, None],
        node_grad[None, None],
        edge_grad[None, None],
        *sums,
    )


def solution(mesh):
    finer = Mesh(mesh.devices.reshape(4, 2, 4, 4), ("lat_0", "lat_1", "lon_0", "lon_1"))
    placed = (
        P(LAT, LON, None, None),
        P(LAT, LON, None, None),
        P(LAT, LON, None),
        P(LAT, LON, None),
        P(LAT, LON),
        P(LAT, LON, None, None),
        P(LAT, LON, None, None),
        P(LAT, LON, None, None),
        P(LAT, LON, None, None),
        P(),
        P(),
        P(),
        P(),
        P(),
        P(),
        P(),
        P(),
    )
    return jax.shard_map(
        shards,
        mesh=finer,
        in_specs=placed,
        out_specs=(
            P(LAT, LON, None, None),
            P(LAT, LON, None, None),
            P(LAT, LON, None, None),
            P(LAT, LON, None, None),
            P(LAT_LON, None),
            P(LAT_LON),
            P(LAT_LON, None),
            P(LAT_LON),
            P(LAT_LON, None),
            P(LAT_LON),
            P(LAT_LON, None),
            P(LAT_LON),
        ),
        check_vma=False,
    )
```

time: 117 us -> 115 us (0.983)
  starting transfers between devices: 38.2 us -> 37 us
    ppermute x0 -> x4, starting transfers between devices: none -> 6.38 us  [swap(): return lax.ppermute(block, axis, pairs + [(j, i) for i, j in pairs])]
    ppermute x4 -> x2, starting transfers between devices: 10.3 us -> 4.92 us  [ring(): lax.ppermute(block, axis, [(i, (i + distance) % n) for i in range(n)])]
    ppermute x4 -> x2, starting transfers between devices: 7.18 us -> 4.32 us  [passed_along(): lax.ppermute(value, axis, [(source, source + steps) for source in range(l...]
    ppermute x0 -> x4, waiting for transfers between devices: none -> 2.04 us  [swap(): return lax.ppermute(block, axis, pairs + [(j, i) for i, j in pairs])]
    ppermute x4 -> x2, waiting for transfers between devices: 1.96 us -> 0.01 us  [passed_along(): lax.ppermute(value, axis, [(source, source + steps) for source in range(l...]
    ppermute x4 -> x2, waiting for transfers between devices: 3.13 us -> 1.2 us  [ring(): lax.ppermute(block, axis, [(i, (i + distance) % n) for i in range(n)])]
    all_to_all x1, waiting for transfers between devices: 7.84 us -> 9.55 us  [shards(): lax.all_to_all(both, ('lat_0', 'lon_0', 'lon_1'), split_axis=0, concat_ax...]
where the time goes in v1:
time: 115 us; the launch traced here: 114 us
  Pallas kernels  51.8 us (45%)
  starting transfers between devices  37 us (32%)
  waiting for transfers between devices  16.8 us (15%)
  other arithmetic  6.03 us (5%)
  between operations  1.47 us (1%)
    pallas_call x1, Pallas kernels, layer(): pl.pallas_call(layer_kernel, name='mesh_layer', in_specs=[pl.BlockSpec(me...  38.2 us
    all_to_all x1, starting transfers between devices, shards(): lax.all_to_all(spread(nodes_l), LAT_LON, split_axis=0, concat_axis=0, til...  11.1 us
    all_to_all x1, waiting for transfers between devices, shards(): lax.all_to_all(both, ('lat_0', 'lon_0', 'lon_1'), split_axis=0, concat_ax...  9.55 us
    pallas_call x1, Pallas kernels, edge_grads(): pl.pallas_call(edge_grad_kernel, name='edge_grads', grid=(STEPS,), in_spe...  8.61 us
    all_to_all x1, starting transfers between devices, shards(): lax.all_to_all(both, ('lat_0', 'lon_0', 'lon_1'), split_axis=0, concat_ax...  6.77 us
    ppermute x4, starting transfers between devices, swap(): return lax.ppermute(block, axis, pairs + [(j, i) for i, j in pairs])  6.38 us
    ppermute x2, starting transfers between devices, ring(): lax.ppermute(block, axis, [(i, (i + distance) % n) for i in range(n)])  4.92 us
    ppermute x2, starting transfers between devices, passed_along(): lax.ppermute(value, axis, [(source, source + steps) for source in range(l...  4.32 us
  transfers between devices with their start and end apart: 11, of which 4 were waited for; matrix products, arithmetic and copies ran while one was open for 2% of the time, Pallas kernels for 9%

profile of v1, /device:TPU:0, one launch (start us, length us, event | category | flops | bytes accessed | tf_op | source)
XLA Modules:
  0.0 114.2 jit_solution(2408533729700071070)
XLA Ops:
  0.6 1.5 %spread_coarse.1 = bf16[128,2,512]{2,1,0:T(2,128)(2,1)} custom-call(bf16[384,512]{1,0:T(8,128)(2,1)} %bitcast.22), custom_call_target="tpu_custom_call" | custom-call | tf_op jit(solution)/shard_map/spread_coarse/pallas_call | solution.py:83
  2.1 11.1 %all-to-all-start = ((bf16[128,2,512]{2,1,0:T(2,128)(2,1)}), bf16[128,2,512]{2,1,0:T(2,128)(2,1)S(1)}, u32[]{:S(2)}, u32[]{:S(2)}) async-start(bf16[128,2,512]{2,1,0:T(2,128)(2,1)} %spread_coarse.1), calls=%async_computation | async-start | bytes 524288 | tf_op jit(solution)/shard_map/all_to_all | solution.py:575
  13.9 0.6 pad_add_fusion.place_ref.count_ref
  14.5 2.0 %border_rows.1 = (bf16[24,512]{1,0:T(8,128)(2,1)}, bf16[24,512]{1,0:T(8,128)(2,1)}, bf16[24,512]{1,0:T(8,128)(2,1)}, bf16[24,512]{1,0:T(8,128)(2,1)}) custom-call(s32[3]{0:T(128)} %pad_add_fusion.place_ref.count_ref, bf16[384,512]{1,0:T(8,128)(2,1)} %bitcast.23, s32[4,24]{1,0:T(4,128)} %bitcast.27), custom_call_target="tpu_custom_call" | custom-call | flops 8589934592 | bytes 8388608 | tf_op jit(solution)/shard_map/border_rows/pallas_call | solution.py:105
  16.6 1.1 collective-permute-start
  17.6 4.6 %collective-permute-start.1 = (bf16[24,512]{1,0:T(8,128)(2,1)}, bf16[24,512]{1,0:T(8,128)(2,1)S(1)}, u32[]{:S(2)}, u32[]{:S(2)}) collective-permute-start(bf16[24,512]{1,0:T(8,128)(2,1)} %get-tuple-element.46), channel_id=1, source_target_pairs={{1,2},{3,4},{5,6},{7,8},{9,10},{11,12},{13,14},{15,0},{2,1},{4,3},... | collective-permute-start | bytes 73736 | tf_op jit(solution)/shard_map/ppermute | solution.py:543
  22.3 0.7 collective-permute-start.3
  23.0 2.0 %collective-permute-done.1.lon_b_ref = bf16[24,512]{1,0:T(8,128)(2,1)S(1)} collective-permute-done((bf16[24,512]{1,0:T(8,128)(2,1)}, bf16[24,512]{1,0:T(8,128)(2,1)S(1)}, u32[]{:S(2)}, u32[]{:S(2)}) %collective-permute-start.1) | collective-permute-done | bytes 24608 | tf_op jit(solution)/shard_map/ppermute | solution.py:543
  25.1 0.6 copy-done.8
  25.8 38.2 %mesh_layer.1 = (bf16[24,512]{1,0:T(8,128)(2,1)}, bf16[24,512]{1,0:T(8,128)(2,1)}, bf16[24,512]{1,0:T(8,128)(2,1)}, bf16[24,512]{1,0:T(8,128)(2,1)}, bf16[384,51...) custom-call(s32[3]{0:T(128)} %pad_add_fusion.place_ref.count_ref, ...), custom_call_target="tpu_custom_call" | custom-call | flops 19327352832 | bytes 31457280 | tf_op jit(solution)/shard_map/mesh_layer/pallas_call | solution.py:415
  64.0 3.4 %collective-permute-start.4 = (bf16[16,128,512]{2,1,0:T(8,128)(2,1)}, bf16[16,128,512]{2,1,0:T(8,128)(2,1)S(1)}, u32[]{:S(2)}, u32[]{:S(2)}) collective-permute-start(bf16[16,128,512]{2,1,0:T(8,128)(2,1)} %get-tuple-element.52), channel_id=1, source_target_pairs={{0,16},{16,0},{1,17},{17,1},{2,18},{18,2},{3,19},{19,3},{4,20},{20... | collective-permute-start | bytes 6291464 | tf_op jit(solution)/shard_map/ppermute | solution.py:610
  67.4 4.0 %collective-permute-done.4 = bf16[16,128,512]{2,1,0:T(8,128)(2,1)S(1)} collective-permute-done((bf16[16,128,512]{2,1,0:T(8,128)(2,1)}, bf16[16,128,512]{2,1,0:T(8,128)(2,1)S(1)}, u32[]{:S(2)}, u32[]{:S(2)}) %collective-permute-start.4) | collective-permute-done | bytes 2097184 | tf_op jit(solution)/shard_map/ppermute | solution.py:610
  71.4 3.5 %add_convert_fusion = bf16[16,128,512]{2,1,0:T(8,128)(2,1)} fusion(bf16[16,128,512]{2,1,0:T(8,128)(2,1)S(1)} %collective-permute-done.4, bf16[16,128,512]{2,1,0:T(8,128)(2,1)} %get-tuple-element.51), kind=kLoop, calls=%fused_computation.1 | loop fusion | flops 4194304 | bytes 6291456 | tf_op jit(solution)/shard_map/convert_element_type | solution.py:611
  74.9 6.8 %all-to-all-start.1 = ((bf16[64,32,512]{2,1,0:T(8,128)(2,1)}), bf16[64,32,512]{2,1,0:T(8,128)(2,1)S(1)}, u32[]{:S(2)}, u32[]{:S(2)}) async-start(bf16[64,32,512]{2,1,0:T(8,128)(2,1)} %bitcast.14), calls=%async_computation.1 | async-start | bytes 4194304 | tf_op jit(solution)/shard_map/all_to_all | solution.py:613
  81.8 4.9 %collective-permute-start.5 = (bf16[24,512]{1,0:T(8,128)(2,1)S(1)}, bf16[24,512]{1,0:T(8,128)(2,1)S(1)}, u32[]{:S(2)}, u32[]{:S(2)}) collective-permute-start(bf16[24,512]{1,0:T(8,128)(2,1)S(1)} %copy-done.6), channel_id=1, source_target_pairs={{0,15},{1,0},{2,1},{3,2},{4,3},{5,4},{6,5},{7,6},{8,7},{9,8},{10,9... | collective-permute-start | bytes 73736 | tf_op jit(solution)/shard_map/ppermute | solution.py:537
  86.7 1.3 %collective-permute-start.7 = (bf16[24,512]{1,0:T(8,128)(2,1)S(1)}, bf16[24,512]{1,0:T(8,128)(2,1)S(1)}, u32[]{:S(2)}, u32[]{:S(2)}) collective-permute-start(bf16[24,512]{1,0:T(8,128)(2,1)S(1)} %copy-done.4), channel_id=1, source_target_pairs={{16,0},{32,16},{48,32},{64,48},{80,64},{96,80},{112,96},{17,1},{33... | collective-permute-start | bytes 73736 | tf_op jit(solution)/shard_map/ppermute | solution.py:549
  88.0 3.0 %collective-permute-start.8 = (bf16[24,512]{1,0:T(8,128)(2,1)S(1)}, bf16[24,512]{1,0:T(8,128)(2,1)S(1)}, u32[]{:S(2)}, u32[]{:S(2)}) collective-permute-start(bf16[24,512]{1,0:T(8,128)(2,1)S(1)} %copy-done.3), channel_id=1, source_target_pairs={{0,16},{16,32},{32,48},{48,64},{64,80},{80,96},{96,112},{1,17},{17... | collective-permute-start | bytes 73736 | tf_op jit(solution)/shard_map/ppermute | solution.py:549
  91.1 8.6 %edge_grads.1 = f32[3072,512]{1,0:T(8,128)} custom-call(s32[3]{0:T(128)} %pad_add_fusion.place_ref.count_ref, s32[3,1,1024]{2,1,0:T(1,128)} %bitcast.26, bf16[3072,512]{1,0:T(8,128)(2,1)} %bitcast.21, bf16[3072,512]{1,0:T(8,128)(2,1)} %get-tuple-element.59.gz_ref, bf16[384,512]{1,0:T(8,128)(2,1)} %get-tuple-element.60.gagg_ref, bf16[1536,512]{1,0:T(8,128)(2,1)} %ew1_ref.1), custom_call_target="tpu_custom_call" | custom-call | flops 2818572288 | bytes 13631488 | tf_op jit(solution)/shard_map/edge_grads/pallas_call | solution.py:477
  99.7 1.2 %collective-permute-done.6 = bf16[24,512]{1,0:T(8,128)(2,1)S(1)} collective-permute-done((bf16[24,512]{1,0:T(8,128)(2,1)S(1)}, bf16[24,512]{1,0:T(8,128)(2,1)S(1)}, u32[]{:S(2)}, u32[]{:S(2)}) %collective-permute-start.6) | collective-permute-done | bytes 24608 | tf_op jit(solution)/shard_map/ppermute | solution.py:537
  100.9 0.3 fusion
  101.2 1.0 add.19.node_ref
  102.2 9.5 %all-to-all-done.1 = bf16[64,32,512]{2,1,0:T(8,128)(2,1)S(1)} async-done(((bf16[64,32,512]{2,1,0:T(8,128)(2,1)}), bf16[64,32,512]{2,1,0:T(8,128)(2,1)S(1)}, u32[]{:S(2)}, u32[]{:S(2)}) %all-to-all-start.1) | async-done | bytes 2097184 | tf_op jit(solution)/shard_map/all_to_all | solution.py:613
  111.7 0.9 convert_reduce_fusion.total_ref
  112.7 1.5 %finish_grads.1 = (f32[384,512]{1,0:T(8,128)}, f32[12,512]{1,0:T(8,128)}, f32[4]{0:T(128)}, f32[4,512]{1,0:T(4,128)}, f32[4]{0:T(128)}, /*index=5*/f32[8,512]{1,...) custom-call(s32[1]{0:T(128)} %bitcast.13.lane_ref, ...), custom_call_target="tpu_custom_call", output_to_operand_aliasing={{0}: (2, {})} | custom-call | tf_op jit(solution)/shard_map/finish_grads/pallas_call | solution.py:519
  (31 shorter events, 0.3 us)
Async XLA Ops:
  2.1 22.9 %all-to-all-start = ((bf16[128,2,512]{2,1,0:T(2,128)(2,1)}), bf16[128,2,512]{2,1,0:T(2,128)(2,1)S(1)}, u32[]{:S(2)}, u32[]{:S(2)}) async-start(bf16[128,2,512]{2,1,0:T(2,128)(2,1)} %spread_coarse.1), calls=%async_computation | async-start | bytes 524288 | tf_op jit(solution)/shard_map/all_to_all | solution.py:575
  16.6 6.4 %collective-permute-start = (bf16[24,512]{1,0:T(8,128)(2,1)}, bf16[24,512]{1,0:T(8,128)(2,1)S(1)}, u32[]{:S(2)}, u32[]{:S(2)}) collective-permute-start(bf16[24,512]{1,0:T(8,128)(2,1)} %get-tuple-element.45), channel_id=1, source_target_pairs={{0,1},{2,3},{4,5},{6,7},{8,9},{10,11},{12,13},{14,15},{1,0},{3,2},... | collective-permute-start | bytes 73736 | tf_op jit(solution)/shard_map/ppermute | solution.py:543
  17.6 7.4 %collective-permute-start.1 = (bf16[24,512]{1,0:T(8,128)(2,1)}, bf16[24,512]{1,0:T(8,128)(2,1)S(1)}, u32[]{:S(2)}, u32[]{:S(2)}) collective-permute-start(bf16[24,512]{1,0:T(8,128)(2,1)} %get-tuple-element.46), channel_id=1, source_target_pairs={{1,2},{3,4},{5,6},{7,8},{9,10},{11,12},{13,14},{15,0},{2,1},{4,3},... | collective-permute-start | bytes 73736 | tf_op jit(solution)/shard_map/ppermute | solution.py:543
  22.3 2.7 %collective-permute-start.2 = (bf16[24,512]{1,0:T(8,128)(2,1)}, bf16[24,512]{1,0:T(8,128)(2,1)S(1)}, u32[]{:S(2)}, u32[]{:S(2)}) collective-permute-start(bf16[24,512]{1,0:T(8,128)(2,1)} %get-tuple-element.47), channel_id=1, source_target_pairs={{0,16},{32,48},{64,80},{96,112},{16,0},{48,32},{80,64},{112,96},{1... | collective-permute-start | bytes 73736 | tf_op jit(solution)/shard_map/ppermute | solution.py:543
  22.3 2.7 %collective-permute-start.3 = (bf16[24,512]{1,0:T(8,128)(2,1)}, bf16[24,512]{1,0:T(8,128)(2,1)S(1)}, u32[]{:S(2)}, u32[]{:S(2)}) collective-permute-start(bf16[24,512]{1,0:T(8,128)(2,1)} %get-tuple-element.48), channel_id=1, source_target_pairs={{16,32},{48,64},{80,96},{32,16},{64,48},{96,80},{17,33},{49,65},{8... | collective-permute-start | bytes 73736 | tf_op jit(solution)/shard_map/ppermute | solution.py:543
  23.0 2.1 %copy-start.7 = (bf16[24,512]{1,0:T(8,128)(2,1)}, bf16[24,512]{1,0:T(8,128)(2,1)S(1)}, u32[]{:S(2)}) copy-start(bf16[24,512]{1,0:T(8,128)(2,1)S(1)} %collective-permute-done.lon_a_ref) | copy-start | bytes 73732
  25.0 0.6 copy-start.8
  25.0 0.6 copy-start.9
  25.0 0.6 copy-start.10
  25.0 0.7 copy-start.1
  64.0 7.4 %collective-permute-start.4 = (bf16[16,128,512]{2,1,0:T(8,128)(2,1)}, bf16[16,128,512]{2,1,0:T(8,128)(2,1)S(1)}, u32[]{:S(2)}, u32[]{:S(2)}) collective-permute-start(bf16[16,128,512]{2,1,0:T(8,128)(2,1)} %get-tuple-element.52), channel_id=1, source_target_pairs={{0,16},{16,0},{1,17},{17,1},{2,18},{18,2},{3,19},{19,3},{4,20},{20... | collective-permute-start | bytes 6291464 | tf_op jit(solution)/shard_map/ppermute | solution.py:610
  74.9 6.8 %copy-start.2 = (s32[1,1,4,24]{3,2,1,0:T(4,128)S(1)}, s32[1,1,4,24]{3,2,1,0:T(4,128)}, u32[]{:S(2)}) copy-start(s32[1,1,4,24]{3,2,1,0:T(4,128)} %param.22) | copy-start | bytes 1156
  74.9 6.9 %copy-start.6 = (bf16[24,512]{1,0:T(8,128)(2,1)S(1)}, bf16[24,512]{1,0:T(8,128)(2,1)}, u32[]{:S(2)}) copy-start(bf16[24,512]{1,0:T(8,128)(2,1)} %get-tuple-element.62) | copy-start | bytes 73732
  74.9 11.8 %copy-start.5 = (bf16[24,512]{1,0:T(8,128)(2,1)S(1)}, bf16[24,512]{1,0:T(8,128)(2,1)}, u32[]{:S(2)}) copy-start(bf16[24,512]{1,0:T(8,128)(2,1)} %get-tuple-element.63) | copy-start | bytes 73732
  74.9 11.8 %copy-start.4 = (bf16[24,512]{1,0:T(8,128)(2,1)S(1)}, bf16[24,512]{1,0:T(8,128)(2,1)}, u32[]{:S(2)}) copy-start(bf16[24,512]{1,0:T(8,128)(2,1)} %get-tuple-element.64) | copy-start | bytes 73732
  74.9 13.1 %copy-start.3 = (bf16[24,512]{1,0:T(8,128)(2,1)S(1)}, bf16[24,512]{1,0:T(8,128)(2,1)}, u32[]{:S(2)}) copy-start(bf16[24,512]{1,0:T(8,128)(2,1)} %get-tuple-element.65) | copy-start | bytes 73732
  74.9 36.8 %all-to-all-start.1 = ((bf16[64,32,512]{2,1,0:T(8,128)(2,1)}), bf16[64,32,512]{2,1,0:T(8,128)(2,1)S(1)}, u32[]{:S(2)}, u32[]{:S(2)}) async-start(bf16[64,32,512]{2,1,0:T(8,128)(2,1)} %bitcast.14), calls=%async_computation.1 | async-start | bytes 4194304 | tf_op jit(solution)/shard_map/all_to_all | solution.py:613
  81.8 17.9 %collective-permute-start.5 = (bf16[24,512]{1,0:T(8,128)(2,1)S(1)}, bf16[24,512]{1,0:T(8,128)(2,1)S(1)}, u32[]{:S(2)}, u32[]{:S(2)}) collective-permute-start(bf16[24,512]{1,0:T(8,128)(2,1)S(1)} %copy-done.6), channel_id=1, source_target_pairs={{0,15},{1,0},{2,1},{3,2},{4,3},{5,4},{6,5},{7,6},{8,7},{9,8},{10,9... | collective-permute-start | bytes 73736 | tf_op jit(solution)/shard_map/ppermute | solution.py:537
  86.7 14.2 %collective-permute-start.6 = (bf16[24,512]{1,0:T(8,128)(2,1)S(1)}, bf16[24,512]{1,0:T(8,128)(2,1)S(1)}, u32[]{:S(2)}, u32[]{:S(2)}) collective-permute-start(bf16[24,512]{1,0:T(8,128)(2,1)S(1)} %copy-done.5), channel_id=1, source_target_pairs={{0,1},{1,2},{2,3},{3,4},{4,5},{5,6},{6,7},{7,8},{8,9},{9,10},{10,1... | collective-permute-start | bytes 73736 | tf_op jit(solution)/shard_map/ppermute | solution.py:537
  86.7 14.2 %collective-permute-start.7 = (bf16[24,512]{1,0:T(8,128)(2,1)S(1)}, bf16[24,512]{1,0:T(8,128)(2,1)S(1)}, u32[]{:S(2)}, u32[]{:S(2)}) collective-permute-start(bf16[24,512]{1,0:T(8,128)(2,1)S(1)} %copy-done.4), channel_id=1, source_target_pairs={{16,0},{32,16},{48,32},{64,48},{80,64},{96,80},{112,96},{17,1},{33... | collective-permute-start | bytes 73736 | tf_op jit(solution)/shard_map/ppermute | solution.py:549
  88.0 12.9 %collective-permute-start.8 = (bf16[24,512]{1,0:T(8,128)(2,1)S(1)}, bf16[24,512]{1,0:T(8,128)(2,1)S(1)}, u32[]{:S(2)}, u32[]{:S(2)}) collective-permute-start(bf16[24,512]{1,0:T(8,128)(2,1)S(1)} %copy-done.3), channel_id=1, source_target_pairs={{0,16},{16,32},{32,48},{48,64},{64,80},{80,96},{96,112},{1,17},{17... | collective-permute-start | bytes 73736 | tf_op jit(solution)/shard_map/ppermute | solution.py:549
  91.1 10.1 %copy-start = (f32[384,512]{1,0:T(8,128)S(1)}, f32[384,512]{1,0:T(8,128)}, u32[]{:S(2)}) copy-start(f32[384,512]{1,0:T(8,128)} %get-tuple-element.61) | copy-start | bytes 2359300

commit v2 on v1

--- a/solution.py
+++ b/solution.py
@@ -73,21 +73,6 @@
     return [
         jnp.where(ids == lane + float(first + 128 * j), 1.0, 0.0).astype(BF) for j in range(chunks)
     ]
-
-
-def spread_kernel(nodes_ref, coarse_ref):
-    coarse_ref[...] = jnp.broadcast_to(nodes_ref[0:COARSE][None], (FAR, COARSE, WIDE))
-
-
-def spread(nodes):
-    return pl.pallas_call(
-        spread_kernel,
-        name="spread_coarse",
-        grid=(1,),
-        in_specs=[pl.BlockSpec((16, WIDE), lambda i: (0, 0))],
-        out_specs=pl.BlockSpec((FAR, COARSE, WIDE), lambda i: (0, 0, 0)),
-        out_shape=jax.ShapeDtypeStruct((FAR, COARSE, WIDE), BF),
-    )(nodes)
 
 
 def border_kernel(place_ref, nodes_ref, rows_ref, *sent_refs):
@@ -183,6 +168,7 @@
     dw2_s,
     gain_s,
     packed_s,
+    half_s,
     whole_sem,
     edges_sem,
     ecot_sem,
@@ -227,14 +213,31 @@
         here = rows_of(i)
         return pltpu.make_async_copy(ecot_s.at[here], gz_hbm.at[here], gz_sem.at[i])
 
-    def packed_out(g):
+    def packed_out(g, half):
         copies = []
         for other, ref in ((0, keep_hbm), (1, send_hbm)):
             group = (g >> 2) * 8 + (place_ref[1] ^ other) * 4 + (g & 3)
+            part = slice(16 * half, 16 * (half + 1))
             copies.append(
-                pltpu.make_async_copy(packed_s.at[group], ref.at[g], packed_sem.at[2 * g + other])
+                pltpu.make_async_copy(
+                    packed_s.at[group, :, part],
+                    ref.at[g, :, part],
+                    packed_sem.at[4 * g + 2 * other + half],
+                )
             )
         return copies
+
+    def pack(half, want):
+        out = lax.broadcasted_iota(jnp.int32, (64, 64), 0)
+        src = lax.broadcasted_iota(jnp.int32, (64, 64), 1)
+        order = jnp.where(src == want(out >> 4, out & 15), 1.0, 0.0).astype(BF)
+        part = slice(16 * half, 16 * (half + 1))
+        for g in range(16):
+            for group in ((g >> 2) * 8 + (g & 3), (g >> 2) * 8 + 4 + (g & 3)):
+                rows = packed_s[group, :, part].reshape(64, WIDE)
+                packed_s[group, :, part] = mm(order, rows).astype(BF).reshape(4, 16, WIDE)
+            for copy in packed_out(g, half):
+                copy.start()
 
     fetch(0).start()
     fetch(1).start()
@@ -271,10 +274,18 @@
     fetch(0).wait()
     table_s[0:NODES] = nodes_ref[...]
     fetch(1).wait()
-    right_s[0:WIDE] = ew1_ref[0:WIDE]
-    right_s[WIDE:FIRST] = mm(table_s[...], ew1_ref[WIDE : 2 * WIDE]).astype(BF)
-    right_s[FIRST:] = mm(nodes_ref[...], ew1_ref[2 * WIDE :]).astype(BF)
+    right_s[0:WIDE] = (ew1_ref[0:WIDE].astype(F32) * 0.5).astype(BF)
+    right_s[WIDE : WIDE + ONES_ROW] = (
+        mm(table_s[0:ONES_ROW], ew1_ref[WIDE : 2 * WIDE]) * 0.5
+    ).astype(BF)
+    bias = eb1_ref[...].reshape(1, WIDE) * 0.5
+    coarse = bias.astype(BF).astype(F32)
+    right_s[WIDE + ONES_ROW : FIRST] = jnp.concatenate(
+        [coarse, bias - coarse, jnp.zeros((30, WIDE), F32)], axis=0
+    ).astype(BF)
+    right_s[FIRST:] = (mm(nodes_ref[...], ew1_ref[2 * WIDE :]) * 0.5).astype(BF)
     fetch(2).wait()
+    half_s[...] = (ew2_ref[...].astype(F32) * 0.5).astype(BF)
 
     def forward(i, carry):
         here = rows_of(i)
@@ -284,21 +295,25 @@
         rcv = jnp.where(slot < count, rcv_ref[i].astype(F32), -1.0)
         hots = hot_lanes(lane_ids(snd), 0, SENDERS // 128)
         lane = lax.broadcasted_iota(jnp.int32, (BLOCK, 128), 1)
-        hots[4] = jnp.where(lane == ONES_ROW - 512, 1.0, hots[4].astype(F32)).astype(BF)
+        hots[4] = jnp.where((lane == ONES_ROW - 512) | (lane == ONES_ROW - 511), 1.0, hots[4].astype(F32)).astype(BF)
         hots += hot_lanes(lane_ids(rcv), 0, NODES // 128)
         for k, hot in enumerate(hots):
             left_s[here, WIDE + 128 * k : WIDE + 128 * (k + 1)] = hot
         edges_in(i).wait()
-        z1 = mm(left_s[here], right_s[...]) + eb1_ref[...].reshape(1, WIDE)
-        act, dact = first_act(z1)
-        act = act.astype(BF)
+        half = mm(left_s[here], right_s[...])
+        t = jnp.tanh(half)
+        up = 1.0 + t
+        act = (half * up).astype(BF)
         act_s[here] = act
-        dact_s[here] = dact.astype(BF)
-        normed, rstd = normalise(mm(act, ew2_ref[...]))
+        dact_s[here] = (up * (1.0 + half * (1.0 - t))).astype(BF)
+        live = lax.broadcasted_iota(jnp.int32, (BLOCK, 1), 0) + at < count
+        z2 = mm(act, ew2_ref[...])
+        centred = z2 - row_mean(z2)
+        rstd = jnp.where(live, lax.rsqrt(row_mean(centred * centred) + EPS), 0.0)
+        normed = centred * rstd
         normed_s[here] = normed.astype(BF)
         rstd_s[here] = jnp.broadcast_to(rstd, (BLOCK, 128))
-        live = (lax.broadcasted_iota(jnp.int32, (BLOCK, 1), 0) + at < count).astype(F32)
-        fresh = (left_s[here, 0:WIDE].astype(F32) + (live * normed) * egain).astype(BF)
+        fresh = (left_s[here, 0:WIDE].astype(F32) + normed * egain).astype(BF)
         fresh_s[here] = fresh
         fresh_out(i).start()
         agg_s[...] += t_mm(left_s[here, FIRST:], fresh)
@@ -325,20 +340,19 @@
     gagg_s[...] = mm_t(gz1, nw1_ref[WIDE:]).astype(BF)
     give(1).start()
     node_s[...] = cot + mm_t(gz1, nw1_ref[0:WIDE])
-    packed_s[0:16, 0:32] = t_mm(nodes, gz1).astype(BF).reshape(16, 32, WIDE)
-    packed_s[16:32, 0:32] = t_mm(agg, gz1).astype(BF).reshape(16, 32, WIDE)
-    packed_s[:, 32:48] = t_mm(act, gz2).astype(BF).reshape(GROUPS, 16, WIDE)
+    packed_s[0:16, 0:2, 0:16] = t_mm(nodes, gz1).astype(BF).reshape(16, 2, 16, WIDE)
+    packed_s[16:32, 0:2, 0:16] = t_mm(agg, gz1).astype(BF).reshape(16, 2, 16, WIDE)
+    packed_s[:, 2, 0:16] = t_mm(act, gz2).astype(BF).reshape(GROUPS, 16, WIDE)
 
     def backward(i, carry):
         here = rows_of(i)
-        live = (lax.broadcasted_iota(jnp.int32, (BLOCK, 1), 0) + i * BLOCK < count).astype(F32)
         ecot_in(i).wait()
-        g = live * ecot_s[here].astype(F32) + mm(left_s[here, FIRST:], gagg_s[...])
+        g = ecot_s[here].astype(F32) + mm(left_s[here, FIRST:], gagg_s[...])
         normed = normed_s[here].astype(F32)
         gain_s[...] += jnp.sum((g * normed).reshape(BLOCK // 8, 8, WIDE), axis=0)
         gz2 = norm_back(g, normed, rstd_s[here][:, 0:1], egain).astype(BF)
         dw2_s[...] += t_mm(act_s[here], gz2)
-        gz1 = (mm_t(gz2, ew2_ref[...]) * dact_s[here].astype(F32)).astype(BF)
+        gz1 = (mm_t(gz2, half_s[...]) * dact_s[here].astype(F32)).astype(BF)
         ecot_s[here] = gz1
         gz_out(i).start()
         dw1_s[...] += t_mm(left_s[here], gz1)
@@ -346,11 +360,17 @@
 
     lax.fori_loop(0, STEPS, backward, 0)
 
+    packed_s[:, 3, 0:16] = dw2_s[...].astype(BF).reshape(GROUPS, 16, WIDE)
+    pack(
+        0,
+        lambda z, slot: jnp.where(
+            slot < 8, 8 * z + slot, jnp.where(slot < 12, 24 + 4 * z + slot, 36 + 4 * z + slot)
+        ),
+    )
     sent, got = dw1_s[WIDE:FIRST].astype(BF), dw1_s[FIRST:].astype(BF)
     back = mm_t(sent, ew1_ref[WIDE : 2 * WIDE])
     node_s[...] += back[0:NODES] + mm_t(got, ew1_ref[2 * WIDE :])
     give(2).start()
-    packed_s[:, 96:112] = dw2_s[...].astype(BF).reshape(GROUPS, 16, WIDE)
     first = jnp.concatenate(
         [
             dw1_s[0:WIDE].astype(BF),
@@ -359,7 +379,7 @@
         ],
         axis=0,
     )
-    packed_s[:, 48:96] = first.reshape(GROUPS, 48, WIDE)
+    packed_s[:, 0:3, 16:32] = first.reshape(GROUPS, 3, 16, WIDE)
     for k, ref in enumerate((east_ref, west_ref, north_ref, south_ref)):
         ref[...] = back[NODES + HALO * k : NODES + HALO * (k + 1)].astype(BF)
     vectors = (
@@ -383,28 +403,20 @@
     high = (slot >= 4) & (slot < 8) & (src == (out >> 4) * 4 + slot - 4) & (need == 1)
     small = (slot >= 8) & (slot < 10) & (src == 120 + slot + (out >> 8) * 2)
     move = jnp.where(low | high | small, 1.0, 0.0).astype(BF)
-    packed_s[:, 112:128] = mm(move, extra.astype(BF)).astype(BF).reshape(GROUPS, 16, WIDE)
-    out = lax.broadcasted_iota(jnp.int32, (128, 128), 0)
-    src = lax.broadcasted_iota(jnp.int32, (128, 128), 1)
-    z, slot = out >> 5, out & 31
-    want = jnp.where(slot < 8, 8 * z + slot, 24 + 4 * z + slot)
-    want = jnp.where(slot >= 12, 36 + 12 * z + slot, want)
-    want = jnp.where(slot >= 24, 72 + 4 * z + slot, want)
-    want = jnp.where(slot >= 28, 112 + z + 4 * (slot - 28), want)
-    want = jnp.where(slot >= 30, 90 + slot, want)
-    order = jnp.where(src == want, 1.0, 0.0).astype(BF)
-    for g in range(16):
-        for group in ((g >> 2) * 8 + (g & 3), (g >> 2) * 8 + 4 + (g & 3)):
-            packed_s[group] = mm(order, packed_s[group]).astype(BF)
-        for copy in packed_out(g):
-            copy.start()
+    packed_s[:, 3, 16:32] = mm(move, extra.astype(BF)).astype(BF).reshape(GROUPS, 16, WIDE)
+    pack(
+        1,
+        lambda z, slot: jnp.where(
+            slot < 12, 12 * z + slot, jnp.where(slot < 14, z + 4 * slot, 42 + slot)
+        ),
+    )
     for k in range(3):
         give(k).wait()
     for i in range(STEPS):
         fresh_out(i).wait()
         gz_out(i).wait()
     for g in range(16):
-        for copy in packed_out(g):
+        for copy in packed_out(g, 0) + packed_out(g, 1):
             copy.wait()
 
 
@@ -425,7 +437,7 @@
             sds((NODES, WIDE), BF),
             sds((NODES, WIDE), F32),
         ]
-        + [sds((16, GROUP_ROWS, WIDE), BF)] * 2,
+        + [sds((16, 4, GROUP_ROWS // 4, WIDE), BF)] * 2,
         scratch_shapes=[
             pltpu.VMEM((NODES, WIDE), BF),
             pltpu.VMEM((NODES, WIDE), BF),
@@ -449,13 +461,14 @@
             pltpu.VMEM((WIDE + TABLE, WIDE), F32),
             pltpu.VMEM((WIDE, WIDE), F32),
             pltpu.VMEM((8, WIDE), F32),
-            pltpu.VMEM((GROUPS, GROUP_ROWS, WIDE), BF),
+            pltpu.VMEM((GROUPS, 4, GROUP_ROWS // 4, WIDE), BF),
+            pltpu.VMEM((WIDE, WIDE), BF),
             pltpu.SemaphoreType.DMA((9,)),
             pltpu.SemaphoreType.DMA((STEPS,)),
             pltpu.SemaphoreType.DMA((STEPS,)),
             pltpu.SemaphoreType.DMA((STEPS,)),
             pltpu.SemaphoreType.DMA((STEPS,)),
-            pltpu.SemaphoreType.DMA((32,)),
+            pltpu.SemaphoreType.DMA((64,)),
         ],
         compiler_params=pltpu.CompilerParams(vmem_limit_bytes=60 * 1024 * 1024),
         cost_estimate=pl.CostEstimate(
@@ -500,8 +513,8 @@
     ew1, eb1, ew2, eg, nw1, nb1, nw2, ng = grads
     nw1[...] = total[0:8]
     nw2[...] = total[8:12]
-    ew1[...] = total[12:24]
-    ew2[...] = total[24:28]
+    ew2[...] = total[12:16]
+    ew1[...] = total[16:28]
     out_ref[...] = node_ref[...]
     out_ref[0:COARSE] += total[28:30]
     half = WIDE // 2
@@ -572,7 +585,8 @@
     rows_out = halo_send[0, 0]
     snd = senders.reshape(STEPS, 1, BLOCK)
     rcv = receivers.reshape(STEPS, 1, BLOCK)
-    far = lax.all_to_all(spread(nodes_l), LAT_LON, split_axis=0, concat_axis=0, tiled=True)
+    far = lax.all_to_all(
+        jnp.broadcast_to(nodes_l[None, :COARSE], (FAR, COARSE, WIDE)), LAT_LON, split_axis=0, concat_axis=0, tiled=True)
     place = jnp.stack(
         [
             edge_count[0, 0],

time: 115 us -> 114 us (level)
  Pallas kernels: 51.8 us -> 48.8 us
  local copies, waits for them, and re-layouts: 0.82 us -> 2.37 us
    pallas_call x1, Pallas kernels: 38.2 us -> 36.7 us  [layer(): pl.pallas_call(layer_kernel, name='mesh_layer', in_specs=[pl.BlockSpec(me...]
    broadcast_in_dim x0 -> x2, local copies, waits for them, and re-layouts: none -> 1.55 us  [shards(): jnp.broadcast_to(nodes_l[None, :COARSE], (FAR, COARSE, WIDE))]
    pallas_call x1 -> x0, Pallas kernels: 1.49 us -> none  [spread(): pl.pallas_call(spread_kernel, name='spread_coarse', grid=(1,), in_specs=[...]
where the time goes in v2:
time: 114 us; the launch traced here: 113 us
  Pallas kernels  48.8 us (43%)
  starting transfers between devices  37 us (32%)
  waiting for transfers between devices  16.8 us (15%)
  other arithmetic  6.32 us (6%)
  local copies, waits for them, and re-layouts  2.37 us (2%)
  between operations  1.47 us (1%)
    pallas_call x1, Pallas kernels, layer(): pl.pallas_call(layer_kernel, name='mesh_layer', in_specs=[pl.BlockSpec(me...  36.7 us
    all_to_all x1, starting transfers between devices, shards(): lax.all_to_all(jnp.broadcast_to(nodes_l[None, :COARSE], (FAR, COARSE, WID...  11.1 us
    all_to_all x1, waiting for transfers between devices, shards(): lax.all_to_all(both, ('lat_0', 'lon_0', 'lon_1'), split_axis=0, concat_ax...  9.54 us
    pallas_call x1, Pallas kernels, edge_grads(): pl.pallas_call(edge_grad_kernel, name='edge_grads', grid=(STEPS,), in_spe...  8.61 us
    all_to_all x1, starting transfers between devices, shards(): lax.all_to_all(both, ('lat_0', 'lon_0', 'lon_1'), split_axis=0, concat_ax...  6.77 us
    ppermute x4, starting transfers between devices, swap(): return lax.ppermute(block, axis, pairs + [(j, i) for i, j in pairs])  6.39 us
    ppermute x2, starting transfers between devices, ring(): lax.ppermute(block, axis, [(i, (i + distance) % n) for i in range(n)])  4.92 us
    ppermute x2, starting transfers between devices, passed_along(): lax.ppermute(value, axis, [(source, source + steps) for source in range(l...  4.32 us
  transfers between devices with their start and end apart: 11, of which 4 were waited for; matrix products, arithmetic and copies ran while one was open for 2% of the time, Pallas kernels for 9%

profile of v2, /device:TPU:0, one launch (start us, length us, event | category | flops | bytes accessed | tf_op | source)
XLA Modules:
  0.0 112.9 jit_solution(10898369211203921696)
XLA Ops:
  0.6 0.7 slice_bitcast_fusion
  1.3 0.8 broadcast_in_dim.21
  2.2 11.1 %all-to-all-start = ((bf16[128,2,512]{2,1,0:T(2,128)(2,1)}), bf16[128,2,512]{2,1,0:T(2,128)(2,1)S(1)}, u32[]{:S(2)}, u32[]{:S(2)}) async-start(bf16[128,2,512]{2,1,0:T(2,128)(2,1)} %broadcast_in_dim.21), calls=%async_computation | async-start | bytes 524288 | tf_op jit(solution)/shard_map/all_to_all | solution.py:588
  14.0 0.6 pad_add_fusion.place_ref.count_ref
  14.6 2.0 %border_rows.1 = (bf16[24,512]{1,0:T(8,128)(2,1)}, bf16[24,512]{1,0:T(8,128)(2,1)}, bf16[24,512]{1,0:T(8,128)(2,1)}, bf16[24,512]{1,0:T(8,128)(2,1)}) custom-call(s32[3]{0:T(128)} %pad_add_fusion.place_ref.count_ref, bf16[384,512]{1,0:T(8,128)(2,1)} %bitcast.27, s32[4,24]{1,0:T(4,128)} %bitcast.26), custom_call_target="tpu_custom_call" | custom-call | flops 8589934592 | bytes 8388608 | tf_op jit(solution)/shard_map/border_rows/pallas_call | solution.py:90
  16.6 1.1 collective-permute-start
  17.7 4.7 %collective-permute-start.1 = (bf16[24,512]{1,0:T(8,128)(2,1)}, bf16[24,512]{1,0:T(8,128)(2,1)S(1)}, u32[]{:S(2)}, u32[]{:S(2)}) collective-permute-start(bf16[24,512]{1,0:T(8,128)(2,1)} %get-tuple-element.46), channel_id=1, source_target_pairs={{1,2},{3,4},{5,6},{7,8},{9,10},{11,12},{13,14},{15,0},{2,1},{4,3},... | collective-permute-start | bytes 73736 | tf_op jit(solution)/shard_map/ppermute | solution.py:556
  22.3 0.7 collective-permute-start.3
  23.0 2.0 %collective-permute-done.1.lon_b_ref = bf16[24,512]{1,0:T(8,128)(2,1)S(1)} collective-permute-done((bf16[24,512]{1,0:T(8,128)(2,1)}, bf16[24,512]{1,0:T(8,128)(2,1)S(1)}, u32[]{:S(2)}, u32[]{:S(2)}) %collective-permute-start.1) | collective-permute-done | bytes 24608 | tf_op jit(solution)/shard_map/ppermute | solution.py:556
  25.1 0.6 copy-done.8
  25.8 36.7 %mesh_layer.1 = (bf16[24,512]{1,0:T(8,128)(2,1)}, bf16[24,512]{1,0:T(8,128)(2,1)}, bf16[24,512]{1,0:T(8,128)(2,1)}, bf16[24,512]{1,0:T(8,128)(2,1)}, bf16[384,51...) custom-call(s32[3]{0:T(128)} %pad_add_fusion.place_ref.count_ref, ...), custom_call_target="tpu_custom_call" | custom-call | flops 19327352832 | bytes 31457280 | tf_op jit(solution)/shard_map/mesh_layer/pallas_call | solution.py:427
  62.5 3.4 %collective-permute-start.4 = (bf16[16,4,32,512]{3,2,1,0:T(8,128)(2,1)}, bf16[16,4,32,512]{3,2,1,0:T(8,128)(2,1)S(1)}, u32[]{:S(2)}, u32[]{:S(2)}) collective-permute-start(bf16[16,4,32,512]{3,2,1,0:T(8,128)(2,1)} %get-tuple-element.52), channel_id=1, source_target_pairs={{0,16},{16,0},{1,17},{17,1},{2,18},{18,2},{3,19},{19,3},{4,20},{20... | collective-permute-start | bytes 6291464 | tf_op jit(solution)/shard_map/ppermute | solution.py:624
  65.9 4.0 %collective-permute-done.4 = bf16[16,4,32,512]{3,2,1,0:T(8,128)(2,1)S(1)} collective-permute-done((bf16[16,4,32,512]{3,2,1,0:T(8,128)(2,1)}, bf16[16,4,32,512]{3,2,1,0:T(8,128)(2,1)S(1)}, u32[]{:S(2)}, u32[]{:S(2)}) %collective-permute-start.4) | collective-permute-done | bytes 2097184 | tf_op jit(solution)/shard_map/ppermute | solution.py:624
  69.9 3.8 %add_convert_fusion = bf16[16,4,32,512]{3,2,1,0:T(8,128)(2,1)} fusion(bf16[16,4,32,512]{3,2,1,0:T(8,128)(2,1)S(1)} %collective-permute-done.4, bf16[16,4,32,512]{3,2,1,0:T(8,128)(2,1)} %get-tuple-element.51), kind=kLoop, calls=%fused_computation.1 | loop fusion | flops 4194304 | bytes 6291456 | tf_op jit(solution)/shard_map/convert_element_type | solution.py:625
  73.7 6.8 %all-to-all-start.1 = ((bf16[64,32,512]{2,1,0:T(8,128)(2,1)}), bf16[64,32,512]{2,1,0:T(8,128)(2,1)S(1)}, u32[]{:S(2)}, u32[]{:S(2)}) async-start(bf16[64,32,512]{2,1,0:T(8,128)(2,1)} %bitcast.15), calls=%async_computation.1 | async-start | bytes 4194304 | tf_op jit(solution)/shard_map/all_to_all | solution.py:627
  80.6 4.9 %collective-permute-start.5 = (bf16[24,512]{1,0:T(8,128)(2,1)S(1)}, bf16[24,512]{1,0:T(8,128)(2,1)S(1)}, u32[]{:S(2)}, u32[]{:S(2)}) collective-permute-start(bf16[24,512]{1,0:T(8,128)(2,1)S(1)} %copy-done.6), channel_id=1, source_target_pairs={{0,15},{1,0},{2,1},{3,2},{4,3},{5,4},{6,5},{7,6},{8,7},{9,8},{10,9... | collective-permute-start | bytes 73736 | tf_op jit(solution)/shard_map/ppermute | solution.py:550
  85.5 1.3 %collective-permute-start.7 = (bf16[24,512]{1,0:T(8,128)(2,1)S(1)}, bf16[24,512]{1,0:T(8,128)(2,1)S(1)}, u32[]{:S(2)}, u32[]{:S(2)}) collective-permute-start(bf16[24,512]{1,0:T(8,128)(2,1)S(1)} %copy-done.4), channel_id=1, source_target_pairs={{16,0},{32,16},{48,32},{64,48},{80,64},{96,80},{112,96},{17,1},{33... | collective-permute-start | bytes 73736 | tf_op jit(solution)/shard_map/ppermute | solution.py:562
  86.8 3.0 %collective-permute-start.8 = (bf16[24,512]{1,0:T(8,128)(2,1)S(1)}, bf16[24,512]{1,0:T(8,128)(2,1)S(1)}, u32[]{:S(2)}, u32[]{:S(2)}) collective-permute-start(bf16[24,512]{1,0:T(8,128)(2,1)S(1)} %copy-done.3), channel_id=1, source_target_pairs={{0,16},{16,32},{32,48},{48,64},{64,80},{80,96},{96,112},{1,17},{17... | collective-permute-start | bytes 73736 | tf_op jit(solution)/shard_map/ppermute | solution.py:562
  89.9 8.6 %edge_grads.1 = f32[3072,512]{1,0:T(8,128)} custom-call(s32[3]{0:T(128)} %pad_add_fusion.place_ref.count_ref, s32[3,1,1024]{2,1,0:T(1,128)} %bitcast.25, bf16[3072,512]{1,0:T(8,128)(2,1)} %bitcast.23, bf16[3072,512]{1,0:T(8,128)(2,1)} %get-tuple-element.59.gz_ref, bf16[384,512]{1,0:T(8,128)(2,1)} %get-tuple-element.60.gagg_ref, bf16[1536,512]{1,0:T(8,128)(2,1)} %ew1_ref.1), custom_call_target="tpu_custom_call" | custom-call | flops 2818572288 | bytes 13631488 | tf_op jit(solution)/shard_map/edge_grads/pallas_call | solution.py:490
  98.5 1.2 %collective-permute-done.6 = bf16[24,512]{1,0:T(8,128)(2,1)S(1)} collective-permute-done((bf16[24,512]{1,0:T(8,128)(2,1)S(1)}, bf16[24,512]{1,0:T(8,128)(2,1)S(1)}, u32[]{:S(2)}, u32[]{:S(2)}) %collective-permute-start.6) | collective-permute-done | bytes 24608 | tf_op jit(solution)/shard_map/ppermute | solution.py:550
  99.9 1.0 add.19.node_ref
  101.0 9.5 %all-to-all-done.1 = bf16[64,32,512]{2,1,0:T(8,128)(2,1)S(1)} async-done(((bf16[64,32,512]{2,1,0:T(8,128)(2,1)}), bf16[64,32,512]{2,1,0:T(8,128)(2,1)S(1)}, u32[]{:S(2)}, u32[]{:S(2)}) %all-to-all-start.1) | async-done | bytes 2097184 | tf_op jit(solution)/shard_map/all_to_all | solution.py:627
  110.5 0.9 convert_reduce_fusion.total_ref
  111.5 1.5 %finish_grads.1 = (f32[384,512]{1,0:T(8,128)}, f32[12,512]{1,0:T(8,128)}, f32[4]{0:T(128)}, f32[4,512]{1,0:T(4,128)}, f32[4]{0:T(128)}, /*index=5*/f32[8,512]{1,...) custom-call(s32[1]{0:T(128)} %bitcast.14.lane_ref, ...), custom_call_target="tpu_custom_call", output_to_operand_aliasing={{0}: (2, {})} | custom-call | tf_op jit(solution)/shard_map/finish_grads/pallas_call | solution.py:532
  (32 shorter events, 0.6 us)
Async XLA Ops:
  2.2 22.9 %all-to-all-start = ((bf16[128,2,512]{2,1,0:T(2,128)(2,1)}), bf16[128,2,512]{2,1,0:T(2,128)(2,1)S(1)}, u32[]{:S(2)}, u32[]{:S(2)}) async-start(bf16[128,2,512]{2,1,0:T(2,128)(2,1)} %broadcast_in_dim.21), calls=%async_computation | async-start | bytes 524288 | tf_op jit(solution)/shard_map/all_to_all | solution.py:588
  16.6 6.4 %collective-permute-start = (bf16[24,512]{1,0:T(8,128)(2,1)}, bf16[24,512]{1,0:T(8,128)(2,1)S(1)}, u32[]{:S(2)}, u32[]{:S(2)}) collective-permute-start(bf16[24,512]{1,0:T(8,128)(2,1)} %get-tuple-element.45), channel_id=1, source_target_pairs={{0,1},{2,3},{4,5},{6,7},{8,9},{10,11},{12,13},{14,15},{1,0},{3,2},... | collective-permute-start | bytes 73736 | tf_op jit(solution)/shard_map/ppermute | solution.py:556
  17.7 7.4 %collective-permute-start.1 = (bf16[24,512]{1,0:T(8,128)(2,1)}, bf16[24,512]{1,0:T(8,128)(2,1)S(1)}, u32[]{:S(2)}, u32[]{:S(2)}) collective-permute-start(bf16[24,512]{1,0:T(8,128)(2,1)} %get-tuple-element.46), channel_id=1, source_target_pairs={{1,2},{3,4},{5,6},{7,8},{9,10},{11,12},{13,14},{15,0},{2,1},{4,3},... | collective-permute-start | bytes 73736 | tf_op jit(solution)/shard_map/ppermute | solution.py:556
  22.3 2.7 %collective-permute-start.2 = (bf16[24,512]{1,0:T(8,128)(2,1)}, bf16[24,512]{1,0:T(8,128)(2,1)S(1)}, u32[]{:S(2)}, u32[]{:S(2)}) collective-permute-start(bf16[24,512]{1,0:T(8,128)(2,1)} %get-tuple-element.47), channel_id=1, source_target_pairs={{0,16},{32,48},{64,80},{96,112},{16,0},{48,32},{80,64},{112,96},{1... | collective-permute-start | bytes 73736 | tf_op jit(solution)/shard_map/ppermute | solution.py:556
  22.3 2.7 %collective-permute-start.3 = (bf16[24,512]{1,0:T(8,128)(2,1)}, bf16[24,512]{1,0:T(8,128)(2,1)S(1)}, u32[]{:S(2)}, u32[]{:S(2)}) collective-permute-start(bf16[24,512]{1,0:T(8,128)(2,1)} %get-tuple-element.48), channel_id=1, source_target_pairs={{16,32},{48,64},{80,96},{32,16},{64,48},{96,80},{17,33},{49,65},{8... | collective-permute-start | bytes 73736 | tf_op jit(solution)/shard_map/ppermute | solution.py:556
  23.0 2.1 %copy-start.7 = (bf16[24,512]{1,0:T(8,128)(2,1)}, bf16[24,512]{1,0:T(8,128)(2,1)S(1)}, u32[]{:S(2)}) copy-start(bf16[24,512]{1,0:T(8,128)(2,1)S(1)} %collective-permute-done.lon_a_ref) | copy-start | bytes 73732
  25.0 0.6 copy-start.8
  25.1 0.6 copy-start.9
  25.1 0.6 copy-start.10
  25.1 0.7 copy-start.1
  62.5 7.4 %collective-permute-start.4 = (bf16[16,4,32,512]{3,2,1,0:T(8,128)(2,1)}, bf16[16,4,32,512]{3,2,1,0:T(8,128)(2,1)S(1)}, u32[]{:S(2)}, u32[]{:S(2)}) collective-permute-start(bf16[16,4,32,512]{3,2,1,0:T(8,128)(2,1)} %get-tuple-element.52), channel_id=1, source_target_pairs={{0,16},{16,0},{1,17},{17,1},{2,18},{18,2},{3,19},{19,3},{4,20},{20... | collective-permute-start | bytes 6291464 | tf_op jit(solution)/shard_map/ppermute | solution.py:624
  73.7 6.8 %copy-start.2 = (s32[1,1,4,24]{3,2,1,0:T(4,128)S(1)}, s32[1,1,4,24]{3,2,1,0:T(4,128)}, u32[]{:S(2)}) copy-start(s32[1,1,4,24]{3,2,1,0:T(4,128)} %param.22) | copy-start | bytes 1156
  73.7 6.9 %copy-start.6 = (bf16[24,512]{1,0:T(8,128)(2,1)S(1)}, bf16[24,512]{1,0:T(8,128)(2,1)}, u32[]{:S(2)}) copy-start(bf16[24,512]{1,0:T(8,128)(2,1)} %get-tuple-element.62) | copy-start | bytes 73732
  73.7 11.8 %copy-start.5 = (bf16[24,512]{1,0:T(8,128)(2,1)S(1)}, bf16[24,512]{1,0:T(8,128)(2,1)}, u32[]{:S(2)}) copy-start(bf16[24,512]{1,0:T(8,128)(2,1)} %get-tuple-element.63) | copy-start | bytes 73732
  73.7 11.8 %copy-start.4 = (bf16[24,512]{1,0:T(8,128)(2,1)S(1)}, bf16[24,512]{1,0:T(8,128)(2,1)}, u32[]{:S(2)}) copy-start(bf16[24,512]{1,0:T(8,128)(2,1)} %get-tuple-element.64) | copy-start | bytes 73732
  73.7 13.1 %copy-start.3 = (bf16[24,512]{1,0:T(8,128)(2,1)S(1)}, bf16[24,512]{1,0:T(8,128)(2,1)}, u32[]{:S(2)}) copy-start(bf16[24,512]{1,0:T(8,128)(2,1)} %get-tuple-element.65) | copy-start | bytes 73732
  73.7 36.8 %all-to-all-start.1 = ((bf16[64,32,512]{2,1,0:T(8,128)(2,1)}), bf16[64,32,512]{2,1,0:T(8,128)(2,1)S(1)}, u32[]{:S(2)}, u32[]{:S(2)}) async-start(bf16[64,32,512]{2,1,0:T(8,128)(2,1)} %bitcast.15), calls=%async_computation.1 | async-start | bytes 4194304 | tf_op jit(solution)/shard_map/all_to_all | solution.py:627
  80.6 17.9 %collective-permute-start.5 = (bf16[24,512]{1,0:T(8,128)(2,1)S(1)}, bf16[24,512]{1,0:T(8,128)(2,1)S(1)}, u32[]{:S(2)}, u32[]{:S(2)}) collective-permute-start(bf16[24,512]{1,0:T(8,128)(2,1)S(1)} %copy-done.6), channel_id=1, source_target_pairs={{0,15},{1,0},{2,1},{3,2},{4,3},{5,4},{6,5},{7,6},{8,7},{9,8},{10,9... | collective-permute-start | bytes 73736 | tf_op jit(solution)/shard_map/ppermute | solution.py:550
  85.5 14.2 %collective-permute-start.6 = (bf16[24,512]{1,0:T(8,128)(2,1)S(1)}, bf16[24,512]{1,0:T(8,128)(2,1)S(1)}, u32[]{:S(2)}, u32[]{:S(2)}) collective-permute-start(bf16[24,512]{1,0:T(8,128)(2,1)S(1)} %copy-done.5), channel_id=1, source_target_pairs={{0,1},{1,2},{2,3},{3,4},{4,5},{5,6},{6,7},{7,8},{8,9},{9,10},{10,1... | collective-permute-start | bytes 73736 | tf_op jit(solution)/shard_map/ppermute | solution.py:550
  85.5 14.2 %collective-permute-start.7 = (bf16[24,512]{1,0:T(8,128)(2,1)S(1)}, bf16[24,512]{1,0:T(8,128)(2,1)S(1)}, u32[]{:S(2)}, u32[]{:S(2)}) collective-permute-start(bf16[24,512]{1,0:T(8,128)(2,1)S(1)} %copy-done.4), channel_id=1, source_target_pairs={{16,0},{32,16},{48,32},{64,48},{80,64},{96,80},{112,96},{17,1},{33... | collective-permute-start | bytes 73736 | tf_op jit(solution)/shard_map/ppermute | solution.py:562
  86.8 12.9 %collective-permute-start.8 = (bf16[24,512]{1,0:T(8,128)(2,1)S(1)}, bf16[24,512]{1,0:T(8,128)(2,1)S(1)}, u32[]{:S(2)}, u32[]{:S(2)}) collective-permute-start(bf16[24,512]{1,0:T(8,128)(2,1)S(1)} %copy-done.3), channel_id=1, source_target_pairs={{0,16},{16,32},{32,48},{48,64},{64,80},{80,96},{96,112},{1,17},{17... | collective-permute-start | bytes 73736 | tf_op jit(solution)/shard_map/ppermute | solution.py:562
  89.9 10.1 %copy-start = (f32[384,512]{1,0:T(8,128)S(1)}, f32[384,512]{1,0:T(8,128)}, u32[]{:S(2)}) copy-start(f32[384,512]{1,0:T(8,128)} %get-tuple-element.61) | copy-start | bytes 2359300

commit v3 on v2

--- a/solution.py
+++ b/solution.py
@@ -134,10 +134,10 @@
     ew2_hbm,
     nw1_hbm,
     nw2_hbm,
-    east_ref,
-    west_ref,
-    north_ref,
-    south_ref,
+    back_lon_a_ref,
+    back_lon_b_ref,
+    back_lat_a_ref,
+    back_lat_b_ref,
     new_nodes_hbm,
     new_edges_hbm,
     gz_hbm,
@@ -380,8 +380,11 @@
         axis=0,
     )
     packed_s[:, 0:3, 16:32] = first.reshape(GROUPS, 3, 16, WIDE)
-    for k, ref in enumerate((east_ref, west_ref, north_ref, south_ref)):
-        ref[...] = back[NODES + HALO * k : NODES + HALO * (k + 1)].astype(BF)
+    to = [back[NODES + HALO * k : NODES + HALO * (k + 1)] for k in range(4)]
+    back_lon_a_ref[...] = jnp.where(odd_lon, to[0], to[1]).astype(BF)
+    back_lon_b_ref[...] = jnp.where(odd_lon, to[1], to[0]).astype(BF)
+    back_lat_a_ref[...] = jnp.where(odd_lat, to[2], to[3]).astype(BF)
+    back_lat_b_ref[...] = jnp.where(odd_lat, to[3], to[2]).astype(BF)
     vectors = (
         dw1_s[WIDE + ONES_ROW : WIDE + ONES_ROW + 1],
         jnp.sum(gain_s[...], axis=0, keepdims=True),
@@ -545,21 +548,10 @@
     )(lane, total, node_grad)
 
 
-def ring(block, axis, distance):
-    n = lax.axis_size(axis)
-    return lax.ppermute(block, axis, [(i, (i + distance) % n) for i in range(n)])
-
-
 def swap(block, axis, first, around):
     n = lax.axis_size(axis)
     pairs = [(i, (i + 1) % n) for i in range(first, n, 2) if around or i + 1 < n]
     return lax.ppermute(block, axis, pairs + [(j, i) for i, j in pairs])
-
-
-def passed_along(value, axis, steps):
-    count = lax.axis_size(axis)
-    leading, last = (max(0, -steps), min(count, count - steps))
-    return lax.ppermute(value, axis, [(source, source + steps) for source in range(leading, last)])
 
 
 def shards(
@@ -629,12 +621,16 @@
     )
     edge_grad = edge_grads(place, rcv, ecot, gz, gagg, e_w1)
     returned = [
-        ring(halo_grad[0], LON, -1),
-        ring(halo_grad[1], LON, 1),
-        passed_along(halo_grad[2], LAT, -1),
-        passed_along(halo_grad[3], LAT, 1),
+        swap(halo_grad[0], LON, 0, True),
+        swap(halo_grad[1], LON, 1, True),
+        swap(halo_grad[2], LAT, 0, False),
+        swap(halo_grad[3], LAT, 1, False),
     ]
-    border = (rows_out.reshape(1, 4 * HALO) == lax.broadcasted_iota(jnp.int32, (NODES, 4 * HALO), 0)).astype(BF)
+    odd = (place[2], 1 - place[2], 2 + place[1], 3 - place[1])
+    sorted_rows = jnp.concatenate(
+        [lax.dynamic_slice_in_dim(rows_out, k, 1, 0) for k in odd], axis=1
+    )
+    border = (sorted_rows == lax.broadcasted_iota(jnp.int32, (NODES, 4 * HALO), 0)).astype(BF)
     node_grad = node_part + jnp.dot(border, jnp.concatenate(returned, axis=0), preferred_element_type=F32)
     parts, edge_grad, node_grad = lax.optimization_barrier((parts, edge_grad, node_grad))
     lane = ((lax.axis_index(LAT_LON) & 63) * 4).astype(jnp.int32).reshape(1)

time: 114 us -> 113 us (level)
  starting transfers between devices: 37 us -> 34.2 us
  waiting for transfers between devices: 16.8 us -> 19.5 us
    ppermute x4 -> x0, starting transfers between devices: 9.25 us -> none  [the longest x2 4.92 us: ring(): lax.ppermute(block, axis, [(i, (i + distance) % n) for i in range(n)])]
    ppermute x4 -> x8, starting transfers between devices: 6.39 us -> 12.8 us  [swap(): return lax.ppermute(block, axis, pairs + [(j, i) for i, j in pairs])]
    ppermute x4 -> x8, waiting for transfers between devices: 2.03 us -> 6 us  [swap(): return lax.ppermute(block, axis, pairs + [(j, i) for i, j in pairs])]
    ppermute x4 -> x0, waiting for transfers between devices: 1.2 us -> none  [the longest x2 1.19 us: ring(): lax.ppermute(block, axis, [(i, (i + distance) % n) for i in range(n)])]
where the time goes in v3:
time: 113 us
  Pallas kernels  48.8 us (43%)
  starting transfers between devices  34.2 us (30%)
  waiting for transfers between devices  19.5 us (17%)
  other arithmetic  6.39 us (6%)
  local copies, waits for them, and re-layouts  2.29 us (2%)
  between operations  1.48 us (1%)
    pallas_call x1, Pallas kernels, layer(): pl.pallas_call(layer_kernel, name='mesh_layer', in_specs=[pl.BlockSpec(me...  36.7 us
    ppermute x8, starting transfers between devices, swap(): return lax.ppermute(block, axis, pairs + [(j, i) for i, j in pairs])  12.8 us
    all_to_all x1, starting transfers between devices, shards(): lax.all_to_all(jnp.broadcast_to(nodes_l[None, :COARSE], (FAR, COARSE, WID...  11.1 us
    all_to_all x1, waiting for transfers between devices, shards(): lax.all_to_all(both, ('lat_0', 'lon_0', 'lon_1'), split_axis=0, concat_ax...  9.54 us
    pallas_call x1, Pallas kernels, edge_grads(): pl.pallas_call(edge_grad_kernel, name='edge_grads', grid=(STEPS,), in_spe...  8.61 us
    all_to_all x1, starting transfers between devices, shards(): lax.all_to_all(both, ('lat_0', 'lon_0', 'lon_1'), split_axis=0, concat_ax...  6.77 us
    ppermute x8, waiting for transfers between devices, swap(): return lax.ppermute(block, axis, pairs + [(j, i) for i, j in pairs])  6 us
    ppermute x1, waiting for transfers between devices, shards(): pair = lax.ppermute(send, 'lat_1', [(0, 1), (1, 0)])  4 us
  transfers between devices with their start and end apart: 11, of which 4 were waited for; matrix products, arithmetic and copies ran while one was open for 2% of the time, Pallas kernels for 9%

profile of v3, /device:TPU:0, one launch (start us, length us, event | category | flops | bytes accessed | tf_op | source)
XLA Modules:
  0.0 112.9 jit_solution(17954035092202904149)
XLA Ops:
  0.6 0.7 slice_bitcast_fusion
  1.3 0.8 broadcast_in_dim.21
  2.2 11.1 %all-to-all-start = ((bf16[128,2,512]{2,1,0:T(2,128)(2,1)}), bf16[128,2,512]{2,1,0:T(2,128)(2,1)S(1)}, u32[]{:S(2)}, u32[]{:S(2)}) async-start(bf16[128,2,512]{2,1,0:T(2,128)(2,1)} %broadcast_in_dim.21), calls=%async_computation | async-start | bytes 524288 | tf_op jit(solution)/shard_map/all_to_all | solution.py:580
  14.0 0.6 pad_add_fusion.place_ref.count_ref
  14.6 2.0 %border_rows.1 = (bf16[24,512]{1,0:T(8,128)(2,1)}, bf16[24,512]{1,0:T(8,128)(2,1)}, bf16[24,512]{1,0:T(8,128)(2,1)}, bf16[24,512]{1,0:T(8,128)(2,1)}) custom-call(s32[3]{0:T(128)} %pad_add_fusion.place_ref.count_ref, bf16[384,512]{1,0:T(8,128)(2,1)} %bitcast.37, s32[4,24]{1,0:T(4,128)} %bitcast.36), custom_call_target="tpu_custom_call" | custom-call | flops 8589934592 | bytes 8388608 | tf_op jit(solution)/shard_map/border_rows/pallas_call | solution.py:90
  16.6 1.1 collective-permute-start
  17.7 4.7 %collective-permute-start.1 = (bf16[24,512]{1,0:T(8,128)(2,1)}, bf16[24,512]{1,0:T(8,128)(2,1)S(1)}, u32[]{:S(2)}, u32[]{:S(2)}) collective-permute-start(bf16[24,512]{1,0:T(8,128)(2,1)} %get-tuple-element.46), channel_id=1, source_target_pairs={{1,2},{3,4},{5,6},{7,8},{9,10},{11,12},{13,14},{15,0},{2,1},{4,3},... | collective-permute-start | bytes 73736 | tf_op jit(solution)/shard_map/ppermute | solution.py:554
  22.3 0.7 collective-permute-start.3
  23.0 2.0 %collective-permute-done.1.lon_b_ref = bf16[24,512]{1,0:T(8,128)(2,1)S(1)} collective-permute-done((bf16[24,512]{1,0:T(8,128)(2,1)}, bf16[24,512]{1,0:T(8,128)(2,1)S(1)}, u32[]{:S(2)}, u32[]{:S(2)}) %collective-permute-start.1) | collective-permute-done | bytes 24608 | tf_op jit(solution)/shard_map/ppermute | solution.py:554
  25.1 0.5 copy-done.8
  25.8 36.7 %mesh_layer.1 = (bf16[24,512]{1,0:T(8,128)(2,1)}, bf16[24,512]{1,0:T(8,128)(2,1)}, bf16[24,512]{1,0:T(8,128)(2,1)}, bf16[24,512]{1,0:T(8,128)(2,1)}, bf16[384,51...) custom-call(s32[3]{0:T(128)} %pad_add_fusion.place_ref.count_ref, ...), custom_call_target="tpu_custom_call" | custom-call | flops 19327352832 | bytes 31457280 | tf_op jit(solution)/shard_map/mesh_layer/pallas_call | solution.py:430
  62.5 3.4 %collective-permute-start.4 = (bf16[16,4,32,512]{3,2,1,0:T(8,128)(2,1)}, bf16[16,4,32,512]{3,2,1,0:T(8,128)(2,1)S(1)}, u32[]{:S(2)}, u32[]{:S(2)}) collective-permute-start(bf16[16,4,32,512]{3,2,1,0:T(8,128)(2,1)} %get-tuple-element.52), channel_id=1, source_target_pairs={{0,16},{16,0},{1,17},{17,1},{2,18},{18,2},{3,19},{19,3},{4,20},{20... | collective-permute-start | bytes 6291464 | tf_op jit(solution)/shard_map/ppermute | solution.py:616
  65.9 4.0 %collective-permute-done.4 = bf16[16,4,32,512]{3,2,1,0:T(8,128)(2,1)S(1)} collective-permute-done((bf16[16,4,32,512]{3,2,1,0:T(8,128)(2,1)}, bf16[16,4,32,512]{3,2,1,0:T(8,128)(2,1)S(1)}, u32[]{:S(2)}, u32[]{:S(2)}) %collective-permute-start.4) | collective-permute-done | bytes 2097184 | tf_op jit(solution)/shard_map/ppermute | solution.py:616
  69.9 3.8 %add_convert_fusion = bf16[16,4,32,512]{3,2,1,0:T(8,128)(2,1)} fusion(bf16[16,4,32,512]{3,2,1,0:T(8,128)(2,1)S(1)} %collective-permute-done.4, bf16[16,4,32,512]{3,2,1,0:T(8,128)(2,1)} %get-tuple-element.51), kind=kLoop, calls=%fused_computation.1 | loop fusion | flops 4194304 | bytes 6291456 | tf_op jit(solution)/shard_map/convert_element_type | solution.py:617
  73.7 6.8 %all-to-all-start.1 = ((bf16[64,32,512]{2,1,0:T(8,128)(2,1)}), bf16[64,32,512]{2,1,0:T(8,128)(2,1)S(1)}, u32[]{:S(2)}, u32[]{:S(2)}) async-start(bf16[64,32,512]{2,1,0:T(8,128)(2,1)} %bitcast.15), calls=%async_computation.1 | async-start | bytes 4194304 | tf_op jit(solution)/shard_map/all_to_all | solution.py:619
  80.6 1.6 %collective-permute-start.5 = (bf16[24,512]{1,0:T(8,128)(2,1)S(1)}, bf16[24,512]{1,0:T(8,128)(2,1)S(1)}, u32[]{:S(2)}, u32[]{:S(2)}) collective-permute-start(bf16[24,512]{1,0:T(8,128)(2,1)S(1)} %copy-done.6), channel_id=1, source_target_pairs={{0,1},{2,3},{4,5},{6,7},{8,9},{10,11},{12,13},{14,15},{1,0},{3,2},... | collective-permute-start | bytes 73736 | tf_op jit(solution)/shard_map/ppermute | solution.py:554
  82.2 4.2 %collective-permute-start.6 = (bf16[24,512]{1,0:T(8,128)(2,1)S(1)}, bf16[24,512]{1,0:T(8,128)(2,1)S(1)}, u32[]{:S(2)}, u32[]{:S(2)}) collective-permute-start(bf16[24,512]{1,0:T(8,128)(2,1)S(1)} %copy-done.5), channel_id=1, source_target_pairs={{1,2},{3,4},{5,6},{7,8},{9,10},{11,12},{13,14},{15,0},{2,1},{4,3},... | collective-permute-start | bytes 73736 | tf_op jit(solution)/shard_map/ppermute | solution.py:554
  86.4 0.7 collective-permute-start.8
  87.1 8.6 %edge_grads.1 = f32[3072,512]{1,0:T(8,128)} custom-call(s32[3]{0:T(128)} %pad_add_fusion.place_ref.count_ref, s32[3,1,1024]{2,1,0:T(1,128)} %bitcast.35, bf16[3072,512]{1,0:T(8,128)(2,1)} %bitcast.33, bf16[3072,512]{1,0:T(8,128)(2,1)} %get-tuple-element.59.gz_ref, bf16[384,512]{1,0:T(8,128)(2,1)} %get-tuple-element.60.gagg_ref, bf16[1536,512]{1,0:T(8,128)(2,1)} %ew1_ref.1), custom_call_target="tpu_custom_call" | custom-call | flops 2818572288 | bytes 13631488 | tf_op jit(solution)/shard_map/edge_grads/pallas_call | solution.py:493
  95.7 4.0 %collective-permute-done.6 = bf16[24,512]{1,0:T(8,128)(2,1)S(1)} collective-permute-done((bf16[24,512]{1,0:T(8,128)(2,1)S(1)}, bf16[24,512]{1,0:T(8,128)(2,1)S(1)}, u32[]{:S(2)}, u32[]{:S(2)}) %collective-permute-start.6) | collective-permute-done | bytes 24608 | tf_op jit(solution)/shard_map/ppermute | solution.py:554
  99.9 1.0 add.39.node_ref
  100.9 9.5 %all-to-all-done.1 = bf16[64,32,512]{2,1,0:T(8,128)(2,1)S(1)} async-done(((bf16[64,32,512]{2,1,0:T(8,128)(2,1)}), bf16[64,32,512]{2,1,0:T(8,128)(2,1)S(1)}, u32[]{:S(2)}, u32[]{:S(2)}) %all-to-all-start.1) | async-done | bytes 2097184 | tf_op jit(solution)/shard_map/all_to_all | solution.py:619
  110.5 0.9 convert_reduce_fusion.total_ref
  111.4 1.5 %finish_grads.1 = (f32[384,512]{1,0:T(8,128)}, f32[12,512]{1,0:T(8,128)}, f32[4]{0:T(128)}, f32[4,512]{1,0:T(4,128)}, f32[4]{0:T(128)}, /*index=5*/f32[8,512]{1,...) custom-call(s32[1]{0:T(128)} %bitcast.14.lane_ref, ...), custom_call_target="tpu_custom_call", output_to_operand_aliasing={{0}: (2, {})} | custom-call | tf_op jit(solution)/shard_map/finish_grads/pallas_call | solution.py:535
  (33 shorter events, 0.6 us)
Async XLA Ops:
  2.2 22.9 %all-to-all-start = ((bf16[128,2,512]{2,1,0:T(2,128)(2,1)}), bf16[128,2,512]{2,1,0:T(2,128)(2,1)S(1)}, u32[]{:S(2)}, u32[]{:S(2)}) async-start(bf16[128,2,512]{2,1,0:T(2,128)(2,1)} %broadcast_in_dim.21), calls=%async_computation | async-start | bytes 524288 | tf_op jit(solution)/shard_map/all_to_all | solution.py:580
  16.6 6.4 %collective-permute-start = (bf16[24,512]{1,0:T(8,128)(2,1)}, bf16[24,512]{1,0:T(8,128)(2,1)S(1)}, u32[]{:S(2)}, u32[]{:S(2)}) collective-permute-start(bf16[24,512]{1,0:T(8,128)(2,1)} %get-tuple-element.45), channel_id=1, source_target_pairs={{0,1},{2,3},{4,5},{6,7},{8,9},{10,11},{12,13},{14,15},{1,0},{3,2},... | collective-permute-start | bytes 73736 | tf_op jit(solution)/shard_map/ppermute | solution.py:554
  17.7 7.4 %collective-permute-start.1 = (bf16[24,512]{1,0:T(8,128)(2,1)}, bf16[24,512]{1,0:T(8,128)(2,1)S(1)}, u32[]{:S(2)}, u32[]{:S(2)}) collective-permute-start(bf16[24,512]{1,0:T(8,128)(2,1)} %get-tuple-element.46), channel_id=1, source_target_pairs={{1,2},{3,4},{5,6},{7,8},{9,10},{11,12},{13,14},{15,0},{2,1},{4,3},... | collective-permute-start | bytes 73736 | tf_op jit(solution)/shard_map/ppermute | solution.py:554
  22.3 2.7 %collective-permute-start.2 = (bf16[24,512]{1,0:T(8,128)(2,1)}, bf16[24,512]{1,0:T(8,128)(2,1)S(1)}, u32[]{:S(2)}, u32[]{:S(2)}) collective-permute-start(bf16[24,512]{1,0:T(8,128)(2,1)} %get-tuple-element.47), channel_id=1, source_target_pairs={{0,16},{32,48},{64,80},{96,112},{16,0},{48,32},{80,64},{112,96},{1... | collective-permute-start | bytes 73736 | tf_op jit(solution)/shard_map/ppermute | solution.py:554
  22.3 2.7 %collective-permute-start.3 = (bf16[24,512]{1,0:T(8,128)(2,1)}, bf16[24,512]{1,0:T(8,128)(2,1)S(1)}, u32[]{:S(2)}, u32[]{:S(2)}) collective-permute-start(bf16[24,512]{1,0:T(8,128)(2,1)} %get-tuple-element.48), channel_id=1, source_target_pairs={{16,32},{48,64},{80,96},{32,16},{64,48},{96,80},{17,33},{49,65},{8... | collective-permute-start | bytes 73736 | tf_op jit(solution)/shard_map/ppermute | solution.py:554
  23.0 2.1 %copy-start.7 = (bf16[24,512]{1,0:T(8,128)(2,1)}, bf16[24,512]{1,0:T(8,128)(2,1)S(1)}, u32[]{:S(2)}) copy-start(bf16[24,512]{1,0:T(8,128)(2,1)S(1)} %collective-permute-done.lon_a_ref) | copy-start | bytes 73732
  25.0 0.6 copy-start.8
  25.1 0.6 copy-start.9
  25.1 0.6 copy-start.10
  25.1 0.7 copy-start.1
  62.5 7.4 %collective-permute-start.4 = (bf16[16,4,32,512]{3,2,1,0:T(8,128)(2,1)}, bf16[16,4,32,512]{3,2,1,0:T(8,128)(2,1)S(1)}, u32[]{:S(2)}, u32[]{:S(2)}) collective-permute-start(bf16[16,4,32,512]{3,2,1,0:T(8,128)(2,1)} %get-tuple-element.52), channel_id=1, source_target_pairs={{0,16},{16,0},{1,17},{17,1},{2,18},{18,2},{3,19},{19,3},{4,20},{20... | collective-permute-start | bytes 6291464 | tf_op jit(solution)/shard_map/ppermute | solution.py:616
  73.7 6.8 %copy-start.2 = (s32[1,1,4,24]{3,2,1,0:T(4,128)S(1)}, s32[1,1,4,24]{3,2,1,0:T(4,128)}, u32[]{:S(2)}) copy-start(s32[1,1,4,24]{3,2,1,0:T(4,128)} %param.22) | copy-start | bytes 1156
  73.7 6.9 %copy-start.6 = (bf16[24,512]{1,0:T(8,128)(2,1)S(1)}, bf16[24,512]{1,0:T(8,128)(2,1)}, u32[]{:S(2)}) copy-start(bf16[24,512]{1,0:T(8,128)(2,1)} %get-tuple-element.62) | copy-start | bytes 73732
  73.7 8.5 %copy-start.5 = (bf16[24,512]{1,0:T(8,128)(2,1)S(1)}, bf16[24,512]{1,0:T(8,128)(2,1)}, u32[]{:S(2)}) copy-start(bf16[24,512]{1,0:T(8,128)(2,1)} %get-tuple-element.63) | copy-start | bytes 73732
  73.7 12.7 %copy-start.4 = (bf16[24,512]{1,0:T(8,128)(2,1)S(1)}, bf16[24,512]{1,0:T(8,128)(2,1)}, u32[]{:S(2)}) copy-start(bf16[24,512]{1,0:T(8,128)(2,1)} %get-tuple-element.64) | copy-start | bytes 73732
  73.7 12.7 %copy-start.3 = (bf16[24,512]{1,0:T(8,128)(2,1)S(1)}, bf16[24,512]{1,0:T(8,128)(2,1)}, u32[]{:S(2)}) copy-start(bf16[24,512]{1,0:T(8,128)(2,1)} %get-tuple-element.65) | copy-start | bytes 73732
  73.7 36.8 %all-to-all-start.1 = ((bf16[64,32,512]{2,1,0:T(8,128)(2,1)}), bf16[64,32,512]{2,1,0:T(8,128)(2,1)S(1)}, u32[]{:S(2)}, u32[]{:S(2)}) async-start(bf16[64,32,512]{2,1,0:T(8,128)(2,1)} %bitcast.15), calls=%async_computation.1 | async-start | bytes 4194304 | tf_op jit(solution)/shard_map/all_to_all | solution.py:619
  80.6 15.1 %collective-permute-start.5 = (bf16[24,512]{1,0:T(8,128)(2,1)S(1)}, bf16[24,512]{1,0:T(8,128)(2,1)S(1)}, u32[]{:S(2)}, u32[]{:S(2)}) collective-permute-start(bf16[24,512]{1,0:T(8,128)(2,1)S(1)} %copy-done.6), channel_id=1, source_target_pairs={{0,1},{2,3},{4,5},{6,7},{8,9},{10,11},{12,13},{14,15},{1,0},{3,2},... | collective-permute-start | bytes 73736 | tf_op jit(solution)/shard_map/ppermute | solution.py:554
  82.2 17.4 %collective-permute-start.6 = (bf16[24,512]{1,0:T(8,128)(2,1)S(1)}, bf16[24,512]{1,0:T(8,128)(2,1)S(1)}, u32[]{:S(2)}, u32[]{:S(2)}) collective-permute-start(bf16[24,512]{1,0:T(8,128)(2,1)S(1)} %copy-done.5), channel_id=1, source_target_pairs={{1,2},{3,4},{5,6},{7,8},{9,10},{11,12},{13,14},{15,0},{2,1},{4,3},... | collective-permute-start | bytes 73736 | tf_op jit(solution)/shard_map/ppermute | solution.py:554
  86.4 13.3 %collective-permute-start.7 = (bf16[24,512]{1,0:T(8,128)(2,1)S(1)}, bf16[24,512]{1,0:T(8,128)(2,1)S(1)}, u32[]{:S(2)}, u32[]{:S(2)}) collective-permute-start(bf16[24,512]{1,0:T(8,128)(2,1)S(1)} %copy-done.4), channel_id=1, source_target_pairs={{0,16},{32,48},{64,80},{96,112},{16,0},{48,32},{80,64},{112,96},{1... | collective-permute-start | bytes 73736 | tf_op jit(solution)/shard_map/ppermute | solution.py:554
  86.4 13.3 %collective-permute-start.8 = (bf16[24,512]{1,0:T(8,128)(2,1)S(1)}, bf16[24,512]{1,0:T(8,128)(2,1)S(1)}, u32[]{:S(2)}, u32[]{:S(2)}) collective-permute-start(bf16[24,512]{1,0:T(8,128)(2,1)S(1)} %copy-done.3), channel_id=1, source_target_pairs={{16,32},{48,64},{80,96},{32,16},{64,48},{96,80},{17,33},{49,65},{8... | collective-permute-start | bytes 73736 | tf_op jit(solution)/shard_map/ppermute | solution.py:554
  87.1 12.9 %copy-start = (f32[384,512]{1,0:T(8,128)S(1)}, f32[384,512]{1,0:T(8,128)}, u32[]{:S(2)}) copy-start(f32[384,512]{1,0:T(8,128)} %get-tuple-element.61) | copy-start | bytes 2359300
